TPU v7x, 512 devices: a whole 4x4x16 slice. The times are simulated.
512 devices in a mesh: head: 8 (over x, core), ctx: 64 (over y, z).
Axes of the slice: x: 4, y: 4, z: 16, core: 2. Of those that a mesh axis runs over, the one named last changes fastest.
Arguments:
- queries: bfloat16 [65536, 2048], P('ctx', 'head'), may hold values from -6 to 6
- key_vectors: bfloat16 [65536, 2048], P('ctx', 'head'), may hold values from -6 to 6
- value_vectors: bfloat16 [65536, 2048], P('ctx', 'head'), may hold values from -6 to 6
- out_grad: bfloat16 [65536, 2048], P('ctx', 'head'), may hold values from -6 to 6
- segment_ids: int32 [65536], P('ctx'), may hold values from 0 to 31, never falling along the last dimension, each value on 1 to 16384 neighbouring positions
- head_gain: float32 [16], P('head'), may hold values from 0.3 to 3
Outputs:
- attended: bfloat16 [65536, 2048], P('ctx', 'head')
- grad_queries: bfloat16 [65536, 2048], P('ctx', 'head')
- grad_keys: bfloat16 [65536, 2048], P('ctx', 'head')
- grad_values: bfloat16 [65536, 2048], P('ctx', 'head')
Inputs may be any that keep to these rules, and one draw needn't show every extreme that they name: `segment_ids`: document numbers never fall along the sequence; every document covers 1 to 16384 positions and one covers exactly 16384.
All inputs are finite; a program needn't handle non-finite values.
Results may differ from a plain program's by a relative error of at most 0.0058.
Values sent between devices are 32-bit elements; how exact they have to be, the bound alone decides.
No kernel may reach another device: no remote copies, remote signals or barrier semaphores. Data moves between devices by JAX's collectives and lax.ppermute only.
A program may use at most 64 MiB of HBM per device.

v0:
```python
import jax
import jax.numpy as jnp
from jax import lax
from jax.sharding import PartitionSpec as P

HEADS = 16
HS = 128


EPS = 1e-05


def entering(value, axis, combine, identity, reverse):
    size, index = (lax.axis_size(axis), lax.axis_index(axis))
    everything = jax.tree.map(lambda part: lax.all_gather(part, axis), value)
    start = jax.tree.map(
        lambda part, zero: jnp.broadcast_to(jnp.asarray(zero, part.dtype), part.shape),
        value,
        identity,
    )

    def turn(k, before):
        at = size - 1 - k if reverse else k
        reached = at > index if reverse else at < index
        new = combine(before, jax.tree.map(lambda part: part[at], everything))
        return jax.tree.map(lambda a, b: jnp.where(reached, a, b), new, before)

    return lax.fori_loop(0, size, turn, start)


def join_forward(earlier, later):
    earlier_none = earlier[0] < 0.0
    later_none = later[0] < 0.0
    joined = (earlier[1] == later[0]) & (later[0] == later[1])
    state = jnp.where(later_none, earlier[2], jnp.where(joined, earlier[2] + later[2], later[2]))
    opening = jnp.where(earlier_none, later[0], earlier[0])
    closing = jnp.where(later_none, earlier[1], later[1])
    return (opening, closing, state)


def join_backward(earlier, later):
    earlier_none = earlier[0] < 0.0
    later_none = later[0] < 0.0
    joined = (later[1] == earlier[0]) & (later[0] == later[1])
    state = jnp.where(later_none, earlier[2], jnp.where(joined, earlier[2] + later[2], later[2]))
    opening = jnp.where(later_none, earlier[0], later[0])
    closing = jnp.where(earlier_none, later[1], earlier[1])
    return (opening, closing, state)


def per_device(queries, key_vectors, value_vectors, out_grad, segment_ids, head_gain):
    row_count = queries.shape[0]
    local_heads = head_gain.shape[0]
    width = HEADS * HS
    layout = (row_count, local_heads, HS)
    query_rows = queries.reshape(layout)
    key_rows = key_vectors.reshape(layout)
    value_rows = value_vectors.reshape(layout)
    opening_id = segment_ids[0]
    closing_id = segment_ids[-1]
    position = jnp.arange(row_count)
    allowed = (
        (position[:, None] >= position[None, :]) & (segment_ids[:, None] == segment_ids[None, :])
    )[None]
    at_open = (segment_ids == opening_id)[:, None, None]
    at_close = (segment_ids == closing_id)[:, None, None]
    zero_half = jnp.zeros((), jnp.bfloat16)
    scores = jnp.einsum("thd,shd->hts", query_rows, key_rows, preferred_element_type=jnp.float32)
    probs = jnp.where(allowed, scores, 0.0).astype(jnp.bfloat16)
    local_out = jnp.einsum("hts,shd->thd", probs, value_rows, preferred_element_type=jnp.float32)
    tail = jnp.einsum(
        "shd,she->hde",
        jnp.where(at_close, key_rows, zero_half),
        value_rows,
        preferred_element_type=jnp.float32,
    )
    open_mark = opening_id.astype(jnp.float32)
    close_mark = closing_id.astype(jnp.float32)
    blank = jnp.zeros_like(tail)
    no_mark = jnp.float32(-1.0)
    prior = entering(
        (open_mark, close_mark, tail), "ctx", join_forward, (no_mark, no_mark, blank), False
    )
    incoming = jnp.where(prior[1] == open_mark, prior[2], 0.0)
    state_in = incoming.astype(jnp.bfloat16)
    carried = jnp.einsum("thd,hde->the", query_rows, state_in, preferred_element_type=jnp.float32)
    attn = local_out + jnp.where(at_open, carried, 0.0)
    gain = head_gain[None, :, None]
    scaled = attn * gain
    grad_rows = out_grad.reshape(layout).astype(jnp.float32)
    power, cross = lax.psum(
        (jnp.sum(scaled * scaled, axis=(1, 2)), jnp.sum(grad_rows * scaled, axis=(1, 2))), "head"
    )
    scale = lax.rsqrt(power / width + EPS)[:, None, None]
    cross = cross[:, None, None]
    attended = (scaled * scale).astype(jnp.bfloat16)
    inner = (gain * (grad_rows * scale - scaled * cross * scale * scale * scale / width)).astype(
        jnp.bfloat16
    )
    dscores = jnp.einsum("the,she->hts", inner, value_rows, preferred_element_type=jnp.float32)
    dprobs = jnp.where(allowed, dscores, 0.0).astype(jnp.bfloat16)
    grad_q = jnp.einsum("hts,shd->thd", dprobs, key_rows, preferred_element_type=jnp.float32)
    grad_q = grad_q + jnp.where(
        at_open,
        jnp.einsum("the,hde->thd", inner, state_in, preferred_element_type=jnp.float32),
        0.0,
    )
    back_tail = jnp.einsum(
        "thd,the->hde",
        jnp.where(at_open, query_rows, zero_half),
        inner,
        preferred_element_type=jnp.float32,
    )
    after = entering(
        (open_mark, close_mark, back_tail), "ctx", join_backward, (no_mark, no_mark, blank), True
    )
    returning = jnp.where(after[0] == close_mark, after[2], 0.0)
    state_grad = returning.astype(jnp.bfloat16)
    grad_k = jnp.einsum("hts,thd->shd", dprobs, query_rows, preferred_element_type=jnp.float32)
    grad_k = grad_k + jnp.where(
        at_close,
        jnp.einsum("hde,she->shd", state_grad, value_rows, preferred_element_type=jnp.float32),
        0.0,
    )
    grad_v = jnp.einsum("hts,the->she", probs, inner, preferred_element_type=jnp.float32)
    grad_v = grad_v + jnp.where(
        at_close,
        jnp.einsum("hde,shd->she", state_grad, key_rows, preferred_element_type=jnp.float32),
        0.0,
    )
    flat = (row_count, local_heads * HS)
    return (
        attended.reshape(flat),
        grad_q.astype(jnp.bfloat16).reshape(flat),
        grad_k.astype(jnp.bfloat16).reshape(flat),
        grad_v.astype(jnp.bfloat16).reshape(flat),
    )


def solution(mesh):
    in_specs = (
        P("ctx", "head"),
        P("ctx", "head"),
        P("ctx", "head"),
        P("ctx", "head"),
        P("ctx"),
        P("head"),
    )
    out_specs = (P("ctx", "head"), P("ctx", "head"), P("ctx", "head"), P("ctx", "head"))
    return jax.shard_map(
        per_device, mesh=mesh, in_specs=in_specs, out_specs=out_specs, check_vma=False
    )
```

profile of v0, /device:TPU:6, one launch (start us, length us, event | category | flops | bytes accessed | tf_op | source)
XLA Modules:
  0.0 1050.8 jit_solution(7796322107653288633)
XLA Ops:
  7.3 1.4 fusion.38
  8.7 1.2 copy.86
  9.9 2.0 broadcast_compare_fusion
  14.3 1.2 copy.59
  15.8 1.3 dynamic-slice
  18.7 150.7 %all-reduce.2 = (f32[64]{0:T(128)S(1)}, f32[64]{0:T(128)S(1)}) all-reduce(f32[64]{0:T(128)S(1)} %dynamic-update-slice, f32[64]{0:T(128)S(1)} %dynamic-update-slice.1), channel_id=1, replica_groups=mesh['head'=8,'ctx'=64] {'ctx'}, use_global_device_ids=true, to_apply=%add | all-reduce | flops 128 | bytes 1024
  170.0 1.6 select_convert_fusion.1
  171.7 1.9 copy-done.1
  173.6 1.5 convolution_bitcast_fusion.2
  175.2 347.5 %while.34 = (s32[]{:T(128)}, f32[]{:T(128)}, f32[2,128,128]{2,1,0:T(8,128)S(1)}, s32[]{:T(128)}, f32[64]{0:T(128)S(1)}, /*index=5*/f32[64]{0:T(128)S(1)}, f32[64...) while((s32[]{:T(128)}, f32[]{:T(128)}, f32[2,128,128]{2,1,0:T(8,128)S(1)}, s32[]{:T(128)}, ...), condition=%wide.region_1.2_spmd.clone, body=%wide.region_0.1_spmd.clone.sunk | while | flops 163850 | bytes 393431 | solution.py:28
  522.6 1.4 multiply_reduce_fusion
  524.1 10.4 all-reduce.3
  534.5 1.6 multiply_convert_fusion
  536.1 1.0 fusion.19
  537.1 1.0 copy.50
  538.1 2.9 select_convert_fusion
  541.0 1.9 copy-done.2
  542.9 1.5 convolution_bitcast_fusion.1
  544.7 1.0 copy.51
  545.7 2.9 fusion.39
  548.7 139.8 %all-gather.7.cloned.1.call-done = f32[128,128,128]{2,1,0:T(8,128)} async-done(((f32[2,128,128]{2,1,0:T(8,128)}), f32[128,128,128]{2,1,0:T(8,128)}) %all-gather.7.cloned.1.call-update) | async-done | bytes 8388624 | tf_op jit(solution)/shard_map/all_gather | solution.py:15
  688.5 347.0 %while.35 = (s32[]{:T(128)}, f32[]{:T(128)}, f32[2,128,128]{2,1,0:T(8,128)S(1)}, s32[]{:T(128)}, f32[64]{0:T(128)S(1)}, /*index=5*/f32[64]{0:T(128)S(1)}, f32[64...) while((s32[]{:T(128)}, f32[]{:T(128)}, ...), condition=%wide.region_7.8_spmd.clone, body=%wide.region_6.7_spmd.clone.sunk | while | flops 163854 | bytes 393501 | solution.py:28
  692.9 1.0 select_select_fusion.5
  698.3 1.0 select_select_fusion.5
  703.7 1.0 select_select_fusion.5
  709.2 1.0 select_select_fusion.5
  714.6 1.0 select_select_fusion.5
  720.0 1.0 select_select_fusion.5
  725.4 1.0 select_select_fusion.5
  747.1 1.0 select_select_fusion.5
  758.0 1.0 select_select_fusion.5
  785.1 1.0 select_select_fusion.5
  795.9 1.0 select_select_fusion.5
  823.0 1.0 select_select_fusion.5
  850.1 1.0 select_select_fusion.5
  861.0 1.0 select_select_fusion.5
  888.1 1.0 select_select_fusion.5
  898.9 1.0 select_select_fusion.5
  926.1 1.0 select_select_fusion.5
  953.2 1.0 select_select_fusion.5
  964.0 1.0 select_select_fusion.5
  991.1 1.0 select_select_fusion.5
  1002.0 1.0 select_select_fusion.5
  1029.1 1.0 select_select_fusion.5
  1035.8 2.2 fusion.10
  1038.0 2.0 copy.53
  1040.0 2.9 fusion.11
  1042.9 1.0 copy.52
  (397 shorter events, 259.8 us)
Async XLA Ops:
  7.2 4.8 copy-start
  7.2 162.2 %copy-start.8 = (s32[1024]{0:T(1024)S(1)}, s32[1024]{0:T(1024)}, u32[]{:S(2)}) copy-start(s32[1024]{0:T(1024)} %param.14) | copy-start | bytes 12292
  7.2 162.8 %copy-start.3 = (bf16[1024,256]{1,0:T(8,128)(2,1)S(1)}, bf16[1024,256]{1,0:T(8,128)(2,1)}, u32[]{:S(2)}) copy-start(bf16[1024,256]{1,0:T(8,128)(2,1)} %param.11) | copy-start | bytes 1572868
  7.2 8.3 copy-start.7
  7.2 167.9 %all-gather.5.cloned.1.call-start = ((), (), s32[]{:S(2)}) async-start(), calls=%async_computation | async-start | bytes 8519680 | tf_op jit(solution)/shard_map/all_gather | solution.py:15
  9.9 4.4 copy-start.4
  12.9 675.5 %all-gather.7.cloned.1.call-start = ((), (), s32[]{:S(2)}) async-start(), calls=%async_computation.1 | async-start | bytes 8519680 | tf_op jit(solution)/shard_map/all_gather | solution.py:15
  170.0 1.6 copy-start.6
  171.7 1.9 copy-start.1
  173.6 349.0 %copy-start.9 = (f32[2]{0:T(128)S(1)}, f32[2]{0:T(128)}, u32[]{:S(2)}) copy-start(f32[2]{0:T(128)} %param.15) | copy-start | bytes 28
  538.1 4.8 copy-start.5
  541.0 2.0 copy-start.2
Sparse Core Ops, SparseCore 0:
  13.0 161.4 all-gather.4
  537.2 151.2 all-gather.6
where the time goes:
time: 1060 us; the launch traced here: 1050 us
  loops' own time  418 us (39%)
  local copies, waits for them, and re-layouts  170 us (16%)
  blocking collectives  161 us (15%)
  waiting for transfers between devices  140 us (13%)
  other arithmetic  127 us (12%)
  matrix products  19.5 us (2%)
  between operations  15.6 us (1%)
    another operation x2, loops' own time, entering(): return lax.fori_loop(0, size, turn, start)  418 us
    dynamic_slice x256, local copies, waits for them, and re-layouts, turn(): new = combine(before, jax.tree.map(lambda part: part[at], everything))  154 us
    unnamed x1, blocking collectives  151 us
    all_gather x2, waiting for transfers between devices, entering(): everything = jax.tree.map(lambda part: lax.all_gather(part, axis), value)  140 us
    select_n x128, other arithmetic, turn(): return jax.tree.map(lambda a, b: jnp.where(reached, a, b), new, before)  123 us
  transfers between devices with their start and end apart: 2, of which 1 were waited for; matrix products, arithmetic and copies ran while one was open for 2% of the time, Pallas kernels for 0%

commit v1 on v0

v1 whole, which is shorter than its diff:
```python
import jax
import jax.numpy as jnp
from jax import lax
from jax.experimental import pallas as pl
from jax.experimental.pallas import tpu as pltpu
from jax.sharding import PartitionSpec as P

HEADS = 16
HS = 128
EPS = 1e-05

ROWS = 1024
LOCAL = 2
N_CTX = 64
STEP = 256
TILES = ROWS // STEP
CHUNK = LOCAL * HS // N_CTX

VMEM = pl.BlockSpec(memory_space=pltpu.VMEM)
SMEM = pl.BlockSpec(memory_space=pltpu.SMEM)
F32 = jnp.float32
BF16 = jnp.bfloat16


def dot(a, b, over, precision=None):
    return lax.dot_general(
        a, b, (((over[0],), (over[1],)), ((), ())), precision=precision, preferred_element_type=F32
    )


def call(kernel, name, outs, gain_last=False):
    def run(*args):
        specs = [VMEM] * (len(args) - 1) + [SMEM if gain_last else VMEM]
        return pl.pallas_call(
            kernel,
            name=name,
            out_shape=[jax.ShapeDtypeStruct(shape, dtype) for shape, dtype in outs],
            in_specs=specs,
            out_specs=[VMEM] * len(outs),
            compiler_params=pltpu.CompilerParams(vmem_limit_bytes=48 << 20),
        )(*args)

    return run


def marks_of(seg_ref):
    seg = seg_ref[...].astype(F32)
    opening, closing = jnp.min(seg), jnp.max(seg)
    n_open = jnp.sum(jnp.where(seg == opening, 1.0, 0.0)).astype(jnp.int32)
    n_close = jnp.sum(jnp.where(seg == closing, 1.0, 0.0)).astype(jnp.int32)
    return opening, closing, n_open, ROWS - n_close


def head_of(ref, h, start=0, size=ROWS):
    return ref[start : start + size, h * HS : (h + 1) * HS]


def positions(start, size):
    return start + lax.broadcasted_iota(jnp.int32, (size, HS), 0)


def put_state(out_ref, states, stride):
    flat = jnp.concatenate(states, axis=0)
    for r in range(CHUNK):
        out_ref[pl.ds(r, N_CTX, stride=stride), :] = flat[r * N_CTX : (r + 1) * N_CTX]


def get_state(ref):
    flat = jnp.concatenate([ref[pl.ds(r, N_CTX, stride=CHUNK), :] for r in range(CHUNK)], axis=0)
    return [flat[h * HS : (h + 1) * HS].astype(BF16) for h in range(LOCAL)]


def tail_kernel(k_ref, v_ref, seg_ref, out_ref):
    opening, closing, _, start = marks_of(seg_ref)
    at_close = positions(0, ROWS) >= start
    tails = []
    for h in range(LOCAL):
        keys = jnp.where(at_close, head_of(k_ref, h).astype(F32), 0.0).astype(BF16)
        tails.append(dot(keys, head_of(v_ref, h), (0, 0)))
    put_state(out_ref, tails, CHUNK + 1)
    lane = lax.broadcasted_iota(jnp.int32, (N_CTX, HS), 1)
    out_ref[pl.ds(CHUNK, N_CTX, stride=CHUNK + 1), :] = jnp.where(lane == 0, opening, closing)


def summed(x_ref, stride, chosen, out_ref):
    x = jnp.concatenate([x_ref[pl.ds(r, N_CTX, stride=stride), :] for r in range(CHUNK)], axis=1)
    y = dot(jnp.where(chosen, 1.0, 0.0), x, (1, 0), lax.Precision.HIGHEST)
    for r in range(CHUNK):
        out_ref[pl.ds(r, N_CTX, stride=CHUNK), :] = y[:, r * HS : (r + 1) * HS]


def square_iota():
    shape = (N_CTX, N_CTX)
    return lax.broadcasted_iota(jnp.int32, shape, 0), lax.broadcasted_iota(jnp.int32, shape, 1)


def as_row(column):
    down, along = square_iota()
    return jnp.sum(jnp.where(down == along, column, 0.0), axis=0, keepdims=True)


def before_kernel(x_ref, out_ref, marks_ref):
    marks = x_ref[pl.ds(CHUNK, N_CTX, stride=CHUNK + 1), :]
    marks_ref[...] = marks
    down, along = square_iota()
    chosen = (along < down) & (as_row(marks[:, 1:2]) == marks[:, 0:1])
    summed(x_ref, CHUNK + 1, chosen, out_ref)


def after_kernel(x_ref, marks_ref, out_ref):
    marks = marks_ref[...]
    down, along = square_iota()
    chosen = (along > down) & (as_row(marks[:, 0:1]) == marks[:, 1:2])
    summed(x_ref, CHUNK, chosen, out_ref)


def column_of(row):
    return jnp.transpose(jnp.broadcast_to(row, (HS, row.shape[1])))


def allowed_tile(seg_ref, i):
    reach = (i + 1) * STEP
    own = column_of(seg_ref[:, i * STEP : reach].astype(F32))
    same = jnp.concatenate([own] * (reach // HS), axis=1) == seg_ref[:, :reach].astype(F32)
    at = i * STEP + lax.broadcasted_iota(jnp.int32, (STEP, reach), 0)
    return same & (lax.broadcasted_iota(jnp.int32, (STEP, reach), 1) <= at)


def local_kernel(q_ref, k_ref, v_ref, row_ref, out_ref):
    for i in range(TILES):
        at, reach = i * STEP, (i + 1) * STEP
        allowed = allowed_tile(row_ref, i)
        for h in range(LOCAL):
            scores = dot(head_of(q_ref, h, at, STEP), head_of(k_ref, h, 0, reach), (1, 1))
            probs = jnp.where(allowed, scores, 0.0).astype(BF16)
            out_ref[at:reach, h * HS : (h + 1) * HS] = dot(
                probs, head_of(v_ref, h, 0, reach), (1, 0)
            )


def attend_kernel(local_ref, q_ref, g_ref, state_ref, seg_ref, gain_ref, scaled_ref, sums_ref):
    _, _, n_open, _ = marks_of(seg_ref)
    states = get_state(state_ref)
    ones = jnp.ones((8, HS), F32)
    for i in range(TILES):
        at, reach = i * STEP, (i + 1) * STEP
        at_open = positions(at, STEP) < n_open
        power = jnp.zeros((STEP, HS), F32)
        cross = jnp.zeros((STEP, HS), F32)
        for h in range(LOCAL):
            carried = dot(head_of(q_ref, h, at, STEP), states[h], (1, 0))
            attn = head_of(local_ref, h, at, STEP) + jnp.where(at_open, carried, 0.0)
            scaled = attn * gain_ref[h]
            scaled_ref[at:reach, h * HS : (h + 1) * HS] = scaled
            power = power + scaled * scaled
            cross = cross + scaled * head_of(g_ref, h, at, STEP).astype(F32)
        sums_ref[0:1, at:reach] = dot(ones, power, (1, 1), lax.Precision.HIGHEST)[0:1]
        sums_ref[1:2, at:reach] = dot(ones, cross, (1, 1), lax.Precision.HIGHEST)[0:1]


def inner_kernel(scaled_ref, g_ref, q_ref, sums_ref, seg_ref, gain_ref, attended_ref, inner_ref, tail_ref):
    _, _, n_open, _ = marks_of(seg_ref)
    width = HEADS * HS
    tails = [jnp.zeros((HS, HS), F32) for _ in range(LOCAL)]
    for i in range(TILES):
        at, reach = i * STEP, (i + 1) * STEP
        scale_row = lax.rsqrt(sums_ref[0:1, at:reach] / width + EPS)
        pull_row = sums_ref[1:2, at:reach] * scale_row * scale_row * scale_row / width
        scale, pull = column_of(scale_row), column_of(pull_row)
        at_open = positions(at, STEP) < n_open
        for h in range(LOCAL):
            cols = slice(h * HS, (h + 1) * HS)
            scaled = scaled_ref[at:reach, cols]
            attended_ref[at:reach, cols] = (scaled * scale).astype(BF16)
            grad = g_ref[at:reach, cols].astype(F32)
            inner = (gain_ref[h] * (grad * scale - scaled * pull)).astype(BF16)
            inner_ref[at:reach, cols] = inner
            query = jnp.where(at_open, q_ref[at:reach, cols].astype(F32), 0.0).astype(BF16)
            tails[h] = tails[h] + dot(query, inner, (0, 0))
    put_state(tail_ref, tails, CHUNK)


def near_queries_kernel(q_ref, k_ref, v_ref, inner_ref, state_ref, seg_ref, row_ref, gq_ref, keys_ref):
    _, _, n_open, _ = marks_of(seg_ref)
    states = get_state(state_ref)
    keys_ref[...] = jnp.zeros(keys_ref.shape, F32)
    for i in range(TILES):
        at, reach = i * STEP, (i + 1) * STEP
        allowed = allowed_tile(row_ref, i)
        at_open = positions(at, STEP) < n_open
        for h in range(LOCAL):
            cols = slice(h * HS, (h + 1) * HS)
            inner = inner_ref[at:reach, cols]
            dscores = dot(inner, v_ref[:reach, cols], (1, 1))
            dprobs = jnp.where(allowed, dscores, 0.0).astype(BF16)
            grad_q = dot(dprobs, k_ref[:reach, cols], (1, 0))
            grad_q = grad_q + jnp.where(at_open, dot(inner, states[h], (1, 1)), 0.0)
            gq_ref[at:reach, cols] = grad_q.astype(BF16)
            keys_ref[:reach, cols] += dot(dprobs, q_ref[at:reach, cols], (0, 0))


def near_values_kernel(q_ref, k_ref, inner_ref, row_ref, values_ref):
    values_ref[...] = jnp.zeros(values_ref.shape, F32)
    for i in range(TILES):
        at, reach = i * STEP, (i + 1) * STEP
        allowed = allowed_tile(row_ref, i)
        for h in range(LOCAL):
            cols = slice(h * HS, (h + 1) * HS)
            scores = dot(q_ref[at:reach, cols], k_ref[:reach, cols], (1, 1))
            probs = jnp.where(allowed, scores, 0.0).astype(BF16)
            values_ref[:reach, cols] += dot(probs, inner_ref[at:reach, cols], (0, 0))


def far_kernel(k_ref, v_ref, keys_ref, values_ref, back_ref, seg_ref, gk_ref, gv_ref):
    _, _, _, start = marks_of(seg_ref)
    backs = get_state(back_ref)
    at_close = positions(0, ROWS) >= start
    for h in range(LOCAL):
        cols = slice(h * HS, (h + 1) * HS)
        far = jnp.where(at_close, dot(v_ref[:, cols], backs[h], (1, 1)), 0.0)
        gk_ref[:, cols] = (keys_ref[:, cols] + far).astype(BF16)
        far = jnp.where(at_close, dot(k_ref[:, cols], backs[h], (1, 0)), 0.0)
        gv_ref[:, cols] = (values_ref[:, cols] + far).astype(BF16)


def exchange(x):
    parts = x.reshape(N_CTX, 1, -1)
    return lax.all_to_all(parts, "ctx", 0, 0, tiled=True).reshape(x.shape)


def over_heads(x):
    pairs = [[2 * i, 2 * i + 1] for i in range(4)]
    rings = [[c + 2 * i for i in range(4)] for c in range(2)]
    x = lax.psum(x, "head", axis_index_groups=pairs)
    return lax.psum(x, "head", axis_index_groups=rings)


def per_device(queries, key_vectors, value_vectors, out_grad, segment_ids, head_gain):
    q, k, v, g, gain = queries, key_vectors, value_vectors, out_grad, head_gain
    seg = segment_ids.reshape(8, HS)
    row = segment_ids.reshape(1, ROWS)
    states = ((N_CTX * CHUNK, HS), F32)
    wide, wide_half = ((ROWS, LOCAL * HS), F32), ((ROWS, LOCAL * HS), BF16)
    payload = ((N_CTX * (CHUNK + 1), HS), F32)

    (tail,) = call(tail_kernel, "tail", [payload])(k, v, seg)
    tails = exchange(tail)
    (local,) = call(local_kernel, "local", [wide])(q, k, v, row)
    before, marks = call(before_kernel, "before", [states, ((N_CTX, HS), F32)])(tails)
    state_in = exchange(before)
    scaled, sums = call(attend_kernel, "attend", [wide, ((2, ROWS), F32)], True)(
        local, q, g, state_in, seg, gain
    )
    sums = over_heads(sums)
    attended, inner, back_tail = call(inner_kernel, "inner", [wide_half, wide_half, states], True)(
        scaled, g, q, sums, seg, gain
    )
    back_tails = exchange(back_tail)
    grad_q, near_k = call(near_queries_kernel, "near_queries", [wide_half, wide])(
        q, k, v, inner, state_in, seg, row
    )
    (after,) = call(after_kernel, "after", [states])(back_tails, marks)
    state_grad = exchange(after)
    (near_v,) = call(near_values_kernel, "near_values", [wide])(q, k, inner, row)
    grad_k, grad_v = call(far_kernel, "far", [wide_half, wide_half])(
        k, v, near_k, near_v, state_grad, seg
    )
    return attended, grad_q, grad_k, grad_v


def solution(mesh):
    both = P("ctx", "head")
    return jax.shard_map(
        per_device,
        mesh=mesh,
        in_specs=(both, both, both, both, P("ctx"), P("head")),
        out_specs=(both, both, both, both),
        check_vma=False,
    )
```

time: 1060 us -> 127 us (0.12)
  the two profiles are of different devices: /device:TPU:6 before, /device:TPU:8 now
where the time goes in v1:
time: 127 us
  blocking collectives  69 us (54%)
  waiting for transfers between devices  18.9 us (15%)
  Pallas kernels  16.7 us (13%)
  starting transfers between devices  13 us (10%)
  local copies, waits for them, and re-layouts  8.26 us (7%)
    all_to_all x2, blocking collectives, exchange(): return lax.all_to_all(parts, 'ctx', 0, 0, tiled=True).reshape(x.shape)  56 us
    all_to_all x2, waiting for transfers between devices, exchange(): return lax.all_to_all(parts, 'ctx', 0, 0, tiled=True).reshape(x.shape)  18.9 us
    pallas_call x9, Pallas kernels, run(): pl.pallas_call(kernel, name=name, out_shape=[jax.ShapeDtypeStruct(shape,...  16.7 us
    all_to_all x2, starting transfers between devices, exchange(): return lax.all_to_all(parts, 'ctx', 0, 0, tiled=True).reshape(x.shape)  13 us
    psum x1, blocking collectives, over_heads(): return lax.psum(x, 'head', axis_index_groups=rings)  10.6 us
    unnamed x30, local copies, waits for them, and re-layouts  8.26 us
  transfers between devices with their start and end apart: 2, of which 2 were waited for; matrix products, arithmetic and copies ran while one was open for 0% of the time, Pallas kernels for 6%

profile of v1, /device:TPU:8, one launch (start us, length us, event | category | flops | bytes accessed | tf_op | source)
XLA Modules:
  0.0 126.6 jit_solution(3938380104886822483)
XLA Ops:
  0.6 0.0 copy-start.1
  0.6 1.0 copy-done.1
  1.7 0.0 copy-start.3
  1.7 1.0 copy-done.3
  2.7 0.0 copy-start.12
  2.7 0.7 copy-done.12
  3.4 0.0 copy-start.2
  3.4 0.0 copy-start.4
  3.4 0.6 tail.1
  4.0 0.0 copy-start
  4.0 35.4 %all_to_all.20 = f32[64,1,640]{2,1,0:T(1,128)S(1)} all-to-all(f32[64,1,640]{2,1,0:T(1,128)S(1)} %bitcast.12), channel_id=1, replica_groups=mesh['head'=8,'ctx'=64] {'ctx'}, dimensions={0} | all-to-all | bytes 327680 | tf_op jit(solution)/shard_map/all_to_all | solution.py:228
  39.4 1.0 before.1
  40.4 0.0 copy-start.13
  40.4 6.7 %all-to-all-start.1 = ((f32[64,1,512]{2,1,0:T(1,128)}), f32[64,1,512]{2,1,0:T(1,128)S(1)}, u32[]{:S(2)}, u32[]{:S(2)}) async-start(f32[64,1,512]{2,1,0:T(1,128)} %bitcast.4), calls=%async_computation.1 | async-start | bytes 262144 | tf_op jit(solution)/shard_map/all_to_all | solution.py:228
  47.1 0.0 copy-done.2
  47.1 0.0 copy-done.4
  47.1 0.0 copy-done
  47.1 0.0 copy-done.13
  47.1 0.0 copy-start.5
  47.2 1.9 %local.1.local_ref = f32[1024,256]{1,0:T(8,128)S(1)} custom-call(bf16[1024,256]{1,0:T(8,128)(2,1)S(1)} %copy-done, bf16[1024,256]{1,0:T(8,128)(2,1)S(1)} %copy-done.2, bf16[1024,256]{1,0:T(8,128)(2,1)S(1)} %copy-done.4, s32[1,1024]{1,0:T(1,128)S(1)} %bitcast.17), custom_call_target="tpu_custom_call" | custom-call | tf_op jit(solution)/shard_map/local/pallas_call | solution.py:34
  49.1 0.0 copy-start.14
  49.1 12.9 %all-to-all-done.1 = f32[64,1,512]{2,1,0:T(1,128)S(1)} async-done(((f32[64,1,512]{2,1,0:T(1,128)}), f32[64,1,512]{2,1,0:T(1,128)S(1)}, u32[]{:S(2)}, u32[]{:S(2)}) %all-to-all-start.1) | async-done | bytes 131104 | tf_op jit(solution)/shard_map/all_to_all | solution.py:228
  61.9 0.0 copy-done.5
  61.9 0.0 copy-done.14
  61.9 2.4 %attend.1 = (f32[1024,256]{1,0:T(8,128)S(1)}, f32[2,1024]{1,0:T(2,128)S(1)}) custom-call(f32[1024,256]{1,0:T(8,128)S(1)} %local.1.local_ref, bf16[1024,256]{1,0:T(8,128)(2,1)S(1)} %copy-done, bf16[1024,256]{1,0:T(8,128)(2,1)S(1)} %copy-done.5, f32[256,128]{1,0:T(8,128)S(1)} %bitcast.10, s32[8,128]{1,0:T(8,128)S(1)} %bitcast.18, f32[2]{0:T(128)S(1)} %copy-done.14), custom_call_target="tpu_custom_call" | custom-call | tf_op jit(solution)/shard_map/attend/pallas_call | solution.py:34
  64.3 0.0 copy-start.8
  64.3 1.0 copy-done.8
  65.3 2.5 %psum.14 = f32[2,1024]{1,0:T(2,128)S(1)} all-reduce(f32[2,1024]{1,0:T(2,128)S(1)} %get-tuple-element.17), channel_id=1, replica_groups={{0,64},{128,192},{256,320},{384,448},{1,65},{129,193},{257,321},{385,44..., use_global_device_ids=true, to_apply=%region_0.0 | all-reduce | flops 2048 | bytes 16384 | tf_op jit(solution)/shard_map/psum | solution.py:234
  67.8 10.6 %psum.15.sums_ref = f32[2,1024]{1,0:T(2,128)S(1)} all-reduce(f32[2,1024]{1,0:T(2,128)S(1)} %psum.14), channel_id=1, replica_groups={{0,128,256,384},{64,192,320,448},{1,129,257,385},{65,193,321,449},{2,13..., use_global_device_ids=true, to_apply=%region_1.0 | all-reduce | flops 2048 | bytes 16384 | tf_op jit(solution)/shard_map/psum | solution.py:235
  78.4 0.0 copy-start.9
  78.4 1.2 copy-done.9
  79.6 2.1 %inner.1 = (bf16[1024,256]{1,0:T(8,128)(2,1)}, bf16[1024,256]{1,0:T(8,128)(2,1)S(1)}, f32[256,128]{1,0:T(8,128)S(1)}) custom-call(f32[1024,256]{1,0:T(8,128)S(1)} %copy-done.9, bf16[1024,256]{1,0:T(8,128)(2,1)S(1)} %copy-done.5, bf16[1024,256]{1,0:T(8,128)(2,1)S(1)} %copy-done, f32[2,1024]{1,0:T(2,128)S(1)} %psum.15.sums_ref, s32[8,128]{1,0:T(8,128)S(1)} %bitcast.19, ...), custom_call_target="tpu_custom_call" | custom-call | tf_op jit(solution)/shard_map/inner/pallas_call | solution.py:34
  81.7 0.0 copy-start.6
  81.7 20.6 %all_to_all.21 = f32[64,1,512]{2,1,0:T(1,128)S(1)} all-to-all(f32[64,1,512]{2,1,0:T(1,128)S(1)} %bitcast.24), channel_id=1, replica_groups=mesh['head'=8,'ctx'=64] {'ctx'}, dimensions={0} | all-to-all | bytes 262144 | tf_op jit(solution)/shard_map/all_to_all | solution.py:228
  102.3 1.0 after.1
  103.3 6.3 %all-to-all-start.3 = ((f32[64,1,512]{2,1,0:T(1,128)}), f32[64,1,512]{2,1,0:T(1,128)S(1)}, u32[]{:S(2)}, u32[]{:S(2)}) async-start(f32[64,1,512]{2,1,0:T(1,128)} %bitcast.8), calls=%async_computation.3 | async-start | bytes 262144 | tf_op jit(solution)/shard_map/all_to_all | solution.py:228
  109.6 0.0 copy-done.6
  109.6 3.8 %near_queries.1 = (bf16[1024,256]{1,0:T(8,128)(2,1)}, f32[1024,256]{1,0:T(8,128)S(1)}) custom-call(bf16[1024,256]{1,0:T(8,128)(2,1)S(1)} %copy-done, bf16[1024,256]{1,0:T(8,128)(2,1)S(1)} %copy-done.2, bf16[1024,256]{1,0:T(8,128)(2,1)S(1)} %copy-done.4, bf16[1024,256]{1,0:T(8,128)(2,1)S(1)} %get-tuple-element.19.inner_ref, f32[256,128]{1,0:T(8,128)S(1)} %bitcast.11, ...), custom_call_target="tpu_custom_call" | custom-call | tf_op jit(solution)/shard_map/near_queries/pallas_call | solution.py:34
  113.4 0.0 copy-start.10
  113.4 1.0 copy-done.10
  114.4 0.0 copy-start.7
  114.4 1.0 copy-done.7
  115.4 2.3 %near_values.1.values_ref = f32[1024,256]{1,0:T(8,128)S(1)} custom-call(bf16[1024,256]{1,0:T(8,128)(2,1)S(1)} %copy-done, bf16[1024,256]{1,0:T(8,128)(2,1)S(1)} %copy-done.2, bf16[1024,256]{1,0:T(8,128)(2,1)S(1)} %copy-done.7, s32[1,1024]{1,0:T(1,128)S(1)} %bitcast.22), custom_call_target="tpu_custom_call" | custom-call | tf_op jit(solution)/shard_map/near_values/pallas_call | solution.py:34
  117.7 6.0 %all-to-all-done.3 = f32[64,1,512]{2,1,0:T(1,128)S(1)} async-done(((f32[64,1,512]{2,1,0:T(1,128)}), f32[64,1,512]{2,1,0:T(1,128)S(1)}, u32[]{:S(2)}, u32[]{:S(2)}) %all-to-all-start.3) | async-done | bytes 131104 | tf_op jit(solution)/shard_map/all_to_all | solution.py:228
  123.8 0.0 copy-start.11
  123.8 1.2 copy-done.11
  125.0 1.6 %far.1 = (bf16[1024,256]{1,0:T(8,128)(2,1)}, bf16[1024,256]{1,0:T(8,128)(2,1)}) custom-call(bf16[1024,256]{1,0:T(8,128)(2,1)S(1)} %copy-done.2, bf16[1024,256]{1,0:T(8,128)(2,1)S(1)} %copy-done.4, f32[1024,256]{1,0:T(8,128)S(1)} %copy-done.11, f32[1024,256]{1,0:T(8,128)S(1)} %near_values.1.values_ref, f32[256,128]{1,0:T(8,128)S(1)} %bitcast.14, ...), custom_call_target="tpu_custom_call" | custom-call | tf_op jit(solution)/shard_map/far/pallas_call | solution.py:34
Async XLA Ops:
  0.6 1.0 copy-start.1
  1.7 1.0 copy-start.3
  2.7 0.7 copy-start.12
  3.4 43.7 %copy-start.2 = (bf16[1024,256]{1,0:T(8,128)(2,1)S(1)}, bf16[1024,256]{1,0:T(8,128)(2,1)}, u32[]{:S(2)}) copy-start(bf16[1024,256]{1,0:T(8,128)(2,1)} %k_ref.9) | copy-start | bytes 1572868
  3.4 43.7 %copy-start.4 = (bf16[1024,256]{1,0:T(8,128)(2,1)S(1)}, bf16[1024,256]{1,0:T(8,128)(2,1)}, u32[]{:S(2)}) copy-start(bf16[1024,256]{1,0:T(8,128)(2,1)} %v_ref.7) | copy-start | bytes 1572868
  4.0 43.1 %copy-start = (bf16[1024,256]{1,0:T(8,128)(2,1)S(1)}, bf16[1024,256]{1,0:T(8,128)(2,1)}, u32[]{:S(2)}) copy-start(bf16[1024,256]{1,0:T(8,128)(2,1)} %q_ref.9) | copy-start | bytes 1572868
  40.4 6.7 %copy-start.13 = (s32[1024]{0:T(1024)S(1)}, s32[1024]{0:T(1024)}, u32[]{:S(2)}) copy-start(s32[1024]{0:T(1024)} %param.10) | copy-start | bytes 12292
  40.4 21.5 %all-to-all-start.1 = ((f32[64,1,512]{2,1,0:T(1,128)}), f32[64,1,512]{2,1,0:T(1,128)S(1)}, u32[]{:S(2)}, u32[]{:S(2)}) async-start(f32[64,1,512]{2,1,0:T(1,128)} %bitcast.4), calls=%async_computation.1 | async-start | bytes 262144 | tf_op jit(solution)/shard_map/all_to_all | solution.py:228
  47.1 14.8 %copy-start.5 = (bf16[1024,256]{1,0:T(8,128)(2,1)S(1)}, bf16[1024,256]{1,0:T(8,128)(2,1)}, u32[]{:S(2)}) copy-start(bf16[1024,256]{1,0:T(8,128)(2,1)} %g_ref.3) | copy-start | bytes 1572868
  49.1 12.9 %copy-start.14 = (f32[2]{0:T(128)S(1)}, f32[2]{0:T(128)}, u32[]{:S(2)}) copy-start(f32[2]{0:T(128)} %gain_ref.3) | copy-start | bytes 28
  64.3 1.0 copy-start.8
  78.4 1.2 copy-start.9
  81.7 27.9 %copy-start.6 = (bf16[1024,256]{1,0:T(8,128)(2,1)}, bf16[1024,256]{1,0:T(8,128)(2,1)S(1)}, u32[]{:S(2)}) copy-start(bf16[1024,256]{1,0:T(8,128)(2,1)S(1)} %get-tuple-element.19.inner_ref) | copy-start | bytes 1572868
  103.3 20.5 %all-to-all-start.3 = ((f32[64,1,512]{2,1,0:T(1,128)}), f32[64,1,512]{2,1,0:T(1,128)S(1)}, u32[]{:S(2)}, u32[]{:S(2)}) async-start(f32[64,1,512]{2,1,0:T(1,128)} %bitcast.8), calls=%async_computation.3 | async-start | bytes 262144 | tf_op jit(solution)/shard_map/all_to_all | solution.py:228
  113.4 1.0 copy-start.10
  114.4 1.0 copy-start.7
  123.8 1.2 copy-start.11

commit v2 on v1

v2 whole, which is shorter than its diff:
```python
import jax
import jax.numpy as jnp
from jax import lax
from jax.experimental import pallas as pl
from jax.experimental.pallas import tpu as pltpu
from jax.sharding import PartitionSpec as P

HEADS = 16
HS = 128
EPS = 1e-05

ROWS = 1024
LOCAL = 2
N_CTX = 64
STEP = 256
TILES = ROWS // STEP
CHUNK = LOCAL * HS // N_CTX

PEERS = 8
LINES = ROWS // HS

VMEM = pl.BlockSpec(memory_space=pltpu.VMEM)
SMEM = pl.BlockSpec(memory_space=pltpu.SMEM)
HBM = pl.BlockSpec(memory_space=pltpu.HBM)
F32 = jnp.float32
BF16 = jnp.bfloat16


def dot(a, b, over):
    return lax.dot_general(
        a, b, (((over[0],), (over[1],)), ((), ())), preferred_element_type=F32
    )


def thirds(x):
    high = x.astype(BF16)
    rest = x - high.astype(F32)
    middle = rest.astype(BF16)
    return [high, middle, (rest - middle.astype(F32)).astype(BF16)]


def together(pairs, sems):
    copies = [pltpu.make_async_copy(a, b, sems.at[i]) for i, (a, b) in enumerate(pairs)]
    for copy in copies:
        copy.start()
    for copy in copies:
        copy.wait()


def staged(kernel, n_in, n_mid, n_out):
    def run(*refs):
        given, rest = refs[:n_in], list(refs[n_in:])
        sems = rest.pop()
        given_held, out_held = rest[n_mid + n_out :][:n_in], rest[n_mid + n_out :][n_in:]
        middle, out = rest[:n_mid], rest[n_mid : n_mid + n_out]
        together(zip(given, given_held), sems)
        kernel(*given_held, *middle, *out_held)
        together(zip(out_held, out), sems)

    return run


def call(kernel, name, outs, far=(), near=(), specs=None, out_far=0, scratch=(), stage=True):
    far = [pltpu.with_memory_space_constraint(x, pltpu.HBM) for x in far]
    if stage and (far or out_far):
        held_outs = outs[len(outs) - out_far :]
        kernel = staged(kernel, len(far), len(near) + len(outs) - out_far, out_far)
        scratch = [pltpu.VMEM(x.shape, x.dtype) for x in far]
        scratch += [pltpu.VMEM(*held) for held in held_outs]
        scratch += [pltpu.SemaphoreType.DMA((len(far) + out_far,))]
    return pl.pallas_call(
        kernel,
        name=name,
        out_shape=[jax.ShapeDtypeStruct(shape, dtype) for shape, dtype in outs],
        in_specs=[HBM] * len(far) + (specs or [VMEM] * len(near)),
        out_specs=[VMEM] * (len(outs) - out_far) + [HBM] * out_far,
        scratch_shapes=list(scratch),
        compiler_params=pltpu.CompilerParams(vmem_limit_bytes=16 << 20),
    )(*far, *near)


def marks_of(seg_ref):
    seg = seg_ref[...].astype(F32)
    opening, closing = jnp.min(seg), jnp.max(seg)
    n_open = jnp.sum(jnp.where(seg == opening, 1.0, 0.0)).astype(jnp.int32)
    n_close = jnp.sum(jnp.where(seg == closing, 1.0, 0.0)).astype(jnp.int32)
    return opening, closing, n_open, ROWS - n_close


def head_of(ref, h, start=0, size=ROWS):
    return ref[start : start + size, h * HS : (h + 1) * HS]


def positions(start, size):
    return start + lax.broadcasted_iota(jnp.int32, (size, HS), 0)


def put_state(out_ref, states, stride):
    flat = jnp.concatenate(states, axis=0)
    for r in range(CHUNK):
        out_ref[pl.ds(r, N_CTX, stride=stride), :] = flat[r * N_CTX : (r + 1) * N_CTX]


def get_state(ref):
    flat = jnp.concatenate([ref[pl.ds(r, N_CTX, stride=CHUNK), :] for r in range(CHUNK)], axis=0)
    return [flat[h * HS : (h + 1) * HS].astype(BF16) for h in range(LOCAL)]


def tail_kernel(seg_hbm, k_hbm, v_hbm, out_ref, seg_ref, k_ref, v_ref, sems, seg_sem):
    def copies(i):
        rows = pl.ds(i * STEP, STEP)
        return [
            pltpu.make_async_copy(k_hbm.at[rows], k_ref.at[rows], sems.at[0, i]),
            pltpu.make_async_copy(v_hbm.at[rows], v_ref.at[rows], sems.at[1, i]),
        ]

    seg_copy = pltpu.make_async_copy(seg_hbm, seg_ref, seg_sem)
    seg_copy.start()
    for i in range(TILES):
        for copy in copies(i):
            copy.start()
    seg_copy.wait()
    opening, closing, _, start = marks_of(seg_ref)
    lane = lax.broadcasted_iota(jnp.int32, (N_CTX, HS), 1)
    out_ref[pl.ds(CHUNK, N_CTX, stride=CHUNK + 1), :] = jnp.where(lane == 0, opening, closing)
    tails = [jnp.zeros((HS, HS), F32) for _ in range(LOCAL)]
    for i in range(TILES):
        for copy in copies(i):
            copy.wait()
        at_close = positions(i * STEP, STEP) >= start
        for h in range(LOCAL):
            keys = head_of(k_ref, h, i * STEP, STEP).astype(F32)
            keys = jnp.where(at_close, keys, 0.0).astype(BF16)
            tails[h] = tails[h] + dot(keys, head_of(v_ref, h, i * STEP, STEP), (0, 0))
    put_state(out_ref, tails, CHUNK + 1)


def summed(x_ref, stride, chosen, out_ref):
    x = jnp.concatenate([x_ref[pl.ds(r, N_CTX, stride=stride), :] for r in range(CHUNK)], axis=1)
    chosen = jnp.where(chosen, 1.0, 0.0).astype(BF16)
    y = dot(jnp.concatenate([chosen] * 3, axis=1), jnp.concatenate(thirds(x), axis=0), (1, 0))
    for r in range(CHUNK):
        out_ref[pl.ds(r, N_CTX, stride=CHUNK), :] = y[:, r * HS : (r + 1) * HS]


def square_iota():
    shape = (N_CTX, N_CTX)
    return lax.broadcasted_iota(jnp.int32, shape, 0), lax.broadcasted_iota(jnp.int32, shape, 1)


def as_row(column):
    down, along = square_iota()
    return jnp.sum(jnp.where(down == along, column, 0.0), axis=0, keepdims=True)


def before_kernel(x_ref, out_ref, marks_ref):
    marks = x_ref[pl.ds(CHUNK, N_CTX, stride=CHUNK + 1), :]
    marks_ref[...] = marks
    down, along = square_iota()
    chosen = (along < down) & (as_row(marks[:, 1:2]) == marks[:, 0:1])
    summed(x_ref, CHUNK + 1, chosen, out_ref)


def after_kernel(x_ref, marks_ref, out_ref):
    marks = marks_ref[...]
    down, along = square_iota()
    chosen = (along > down) & (as_row(marks[:, 0:1]) == marks[:, 1:2])
    summed(x_ref, CHUNK, chosen, out_ref)


def column_of(row):
    return jnp.transpose(jnp.broadcast_to(row, (HS, row.shape[1])))


def allowed_tile(seg_ref, i):
    reach = (i + 1) * STEP
    own = column_of(seg_ref[:, i * STEP : reach].astype(F32))
    same = jnp.concatenate([own] * (reach // HS), axis=1) == seg_ref[:, :reach].astype(F32)
    at = i * STEP + lax.broadcasted_iota(jnp.int32, (STEP, reach), 0)
    return same & (lax.broadcasted_iota(jnp.int32, (STEP, reach), 1) <= at)


def local_kernel(q_ref, k_ref, v_ref, seg_ref, row_ref, gain_ref, out_ref, open_ref, gains_ref):
    _, _, n_open, _ = marks_of(seg_ref)
    for h in range(LOCAL):
        gains_ref[h : h + 1, :] = jnp.full((1, HS), gain_ref[h], F32)
    for i in range(TILES):
        at, reach = i * STEP, (i + 1) * STEP
        allowed = allowed_tile(row_ref, i)
        at_open = positions(at, STEP) < n_open
        for h in range(LOCAL):
            cols = slice(h * HS, (h + 1) * HS)
            query = q_ref[at:reach, cols]
            scores = dot(query, head_of(k_ref, h, 0, reach), (1, 1))
            probs = jnp.where(allowed, scores, 0.0).astype(BF16)
            out_ref[at:reach, cols] = dot(probs, head_of(v_ref, h, 0, reach), (1, 0))
            open_ref[at:reach, cols] = jnp.where(at_open, query.astype(F32), 0.0).astype(BF16)


def line_of(x):
    ones = jnp.ones((8, 3 * HS), BF16)
    return dot(ones, jnp.concatenate(thirds(x), axis=1), (1, 1))[0:1]


def attend_kernel(g_hbm, local_ref, open_ref, state_ref, gain_ref, scaled_ref, sums_ref, g_ref, sems):
    def copy(i):
        rows = pl.ds(i * STEP, STEP)
        return pltpu.make_async_copy(g_hbm.at[rows], g_ref.at[rows], sems.at[i])

    for i in range(TILES):
        copy(i).start()
    states = get_state(state_ref)
    for i in range(TILES):
        at, reach = i * STEP, (i + 1) * STEP
        power = jnp.zeros((STEP, HS), F32)
        cross = jnp.zeros((STEP, HS), F32)
        copy(i).wait()
        for h in range(LOCAL):
            carried = dot(head_of(open_ref, h, at, STEP), states[h], (1, 0))
            scaled = (head_of(local_ref, h, at, STEP) + carried) * gain_ref[h : h + 1, :]
            scaled_ref[at:reach, h * HS : (h + 1) * HS] = scaled
            power = power + scaled * scaled
            cross = cross + scaled * head_of(g_ref, h, at, STEP).astype(F32)
        for n, line in enumerate((line_of(power), line_of(cross))):
            for j in range(STEP // HS):
                own = line[:, j * HS : (j + 1) * HS]
                first = n * LINES + i * (STEP // HS) + j
                for peer in range(PEERS):
                    sums_ref[peer * 2 * LINES + first : peer * 2 * LINES + first + 1, :] = own


def scale_and_pull(sums_ref):
    lines = 2 * LINES
    total = sums_ref[0:lines]
    for peer in range(1, PEERS):
        total = total + sums_ref[peer * lines : (peer + 1) * lines]
    width = HEADS * HS
    scale = lax.rsqrt(total[:LINES] / width + EPS)
    return scale, total[LINES:] * scale * scale * scale / width


def columns_of(lines, i):
    per = STEP // HS
    return jnp.concatenate([column_of(lines[i * per + j : i * per + j + 1]) for j in range(per)], axis=0)


def inner_kernel(scaled_ref, g_ref, open_ref, sums_ref, gain_ref, inner_ref, tail_ref):
    scale, pull = scale_and_pull(sums_ref)
    tails = [jnp.zeros((HS, HS), F32) for _ in range(LOCAL)]
    for i in range(TILES):
        at, reach = i * STEP, (i + 1) * STEP
        scales, pulls = columns_of(scale, i), columns_of(pull, i)
        for h in range(LOCAL):
            cols = slice(h * HS, (h + 1) * HS)
            grad = g_ref[at:reach, cols].astype(F32)
            inner = (gain_ref[h : h + 1, :] * (grad * scales - scaled_ref[at:reach, cols] * pulls)).astype(BF16)
            inner_ref[at:reach, cols] = inner
            tails[h] = tails[h] + dot(open_ref[at:reach, cols], inner, (0, 0))
    put_state(tail_ref, tails, CHUNK)


def attended_kernel(scaled_ref, sums_ref, out_ref):
    scale, _ = scale_and_pull(sums_ref)
    for i in range(TILES):
        at, reach = i * STEP, (i + 1) * STEP
        scales = columns_of(scale, i)
        for h in range(LOCAL):
            cols = slice(h * HS, (h + 1) * HS)
            out_ref[at:reach, cols] = (scaled_ref[at:reach, cols] * scales).astype(BF16)


def near_queries_kernel(q_ref, k_ref, v_ref, seg_ref, row_ref, inner_ref, state_ref, gq_ref, keys_ref):
    _, _, n_open, _ = marks_of(seg_ref)
    states = get_state(state_ref)
    keys_ref[...] = jnp.zeros(keys_ref.shape, F32)
    for i in range(TILES):
        at, reach = i * STEP, (i + 1) * STEP
        allowed = allowed_tile(row_ref, i)
        at_open = positions(at, STEP) < n_open
        for h in range(LOCAL):
            cols = slice(h * HS, (h + 1) * HS)
            inner = inner_ref[at:reach, cols]
            dscores = dot(inner, v_ref[:reach, cols], (1, 1))
            dprobs = jnp.where(allowed, dscores, 0.0).astype(BF16)
            grad_q = dot(dprobs, k_ref[:reach, cols], (1, 0))
            grad_q = grad_q + jnp.where(at_open, dot(inner, states[h], (1, 1)), 0.0)
            gq_ref[at:reach, cols] = grad_q.astype(BF16)
            keys_ref[:reach, cols] += dot(dprobs, q_ref[at:reach, cols], (0, 0))


def near_values_kernel(q_ref, k_ref, row_ref, inner_ref, values_ref):
    values_ref[...] = jnp.zeros(values_ref.shape, F32)
    for i in range(TILES):
        at, reach = i * STEP, (i + 1) * STEP
        allowed = allowed_tile(row_ref, i)
        for h in range(LOCAL):
            cols = slice(h * HS, (h + 1) * HS)
            scores = dot(q_ref[at:reach, cols], k_ref[:reach, cols], (1, 1))
            probs = jnp.where(allowed, scores, 0.0).astype(BF16)
            values_ref[:reach, cols] += dot(probs, inner_ref[at:reach, cols], (0, 0))


def far_kernel(
    values_hbm, k_ref, v_ref, keys_ref, back_ref, seg_ref, gk_hbm, gv_hbm, values_ref, gk_ref, gv_ref, sems
):
    def copy(n, a, b, i):
        rows = pl.ds(i * STEP, STEP)
        return pltpu.make_async_copy(a.at[rows], b.at[rows], sems.at[n, i])

    for i in range(TILES):
        copy(0, values_hbm, values_ref, i).start()
    _, _, _, start = marks_of(seg_ref)
    backs = get_state(back_ref)
    for i in range(TILES):
        at, reach = i * STEP, (i + 1) * STEP
        at_close = positions(at, STEP) >= start
        for h in range(LOCAL):
            cols = slice(h * HS, (h + 1) * HS)
            far = jnp.where(at_close, dot(v_ref[at:reach, cols], backs[h], (1, 1)), 0.0)
            gk_ref[at:reach, cols] = (keys_ref[at:reach, cols] + far).astype(BF16)
        copy(1, gk_ref, gk_hbm, i).start()
    for i in range(TILES):
        at, reach = i * STEP, (i + 1) * STEP
        at_close = positions(at, STEP) >= start
        copy(0, values_hbm, values_ref, i).wait()
        for h in range(LOCAL):
            cols = slice(h * HS, (h + 1) * HS)
            far = jnp.where(at_close, dot(k_ref[at:reach, cols], backs[h], (1, 0)), 0.0)
            gv_ref[at:reach, cols] = (values_ref[at:reach, cols] + far).astype(BF16)
        copy(2, gv_ref, gv_hbm, i).start()
    for i in range(TILES):
        copy(1, gk_ref, gk_hbm, i).wait()
        copy(2, gv_ref, gv_hbm, i).wait()


def exchange(x):
    parts = x.reshape(N_CTX, 1, -1)
    return lax.all_to_all(parts, "ctx", 0, 0, tiled=True).reshape(x.shape)


def over_heads(x):
    parts = x.reshape(PEERS, 1, -1)
    return lax.all_to_all(parts, "head", 0, 0, tiled=True).reshape(x.shape)


def per_device(queries, key_vectors, value_vectors, out_grad, segment_ids, head_gain):
    q, k, v, g, gain = queries, key_vectors, value_vectors, out_grad, head_gain
    seg = segment_ids.reshape(8, HS)
    row = segment_ids.reshape(1, ROWS)
    states = ((N_CTX * CHUNK, HS), F32)
    wide, wide_half = ((ROWS, LOCAL * HS), F32), ((ROWS, LOCAL * HS), BF16)
    payload = ((N_CTX * (CHUNK + 1), HS), F32)
    sums = ((PEERS * 2 * LINES, HS), F32)
    half_stage = pltpu.VMEM(*wide_half)
    two = [half_stage, half_stage, pltpu.SemaphoreType.DMA((2, TILES))]

    seg_stage, seg_sem = pltpu.VMEM((8, HS), jnp.int32), pltpu.SemaphoreType.DMA
    (tail,) = call(
        tail_kernel, "tail", [payload], (seg, k, v), scratch=[seg_stage, *two, seg_sem], stage=False
    )
    tails = exchange(tail)
    gains = ((LOCAL, HS), F32)
    local, q_open, gains = call(
        local_kernel, "local", [wide, wide_half, gains], (q, k, v, seg, row), (gain,), [SMEM]
    )
    before, marks = call(before_kernel, "before", [states, ((N_CTX, HS), F32)], near=(tails,))
    state_in = exchange(before)
    scaled, part = call(
        attend_kernel,
        "attend",
        [wide, sums],
        (g,),
        (local, q_open, state_in, gains),
        scratch=[half_stage, pltpu.SemaphoreType.DMA((TILES,))],
        stage=False,
    )
    total = over_heads(part)
    inner, back_tail = call(
        inner_kernel, "inner", [wide_half, states], (), (scaled, g, q_open, total, gains)
    )
    back_tails = exchange(back_tail)
    (attended,) = call(attended_kernel, "attended", [wide_half], near=(scaled, total))
    grad_q, near_k = call(
        near_queries_kernel, "near_queries", [wide_half, wide], (q, k, v, seg, row), (inner, state_in)
    )
    (after,) = call(after_kernel, "after", [states], near=(back_tails, marks))
    state_grad = exchange(after)
    (near_v,) = call(near_values_kernel, "near_values", [wide], (q, k, row), (inner,), out_far=1)
    grad_k, grad_v = call(
        far_kernel,
        "far",
        [wide_half, wide_half],
        (near_v,),
        (k, v, near_k, state_grad, seg),
        out_far=2,
        scratch=[pltpu.VMEM(*wide), half_stage, half_stage, pltpu.SemaphoreType.DMA((3, TILES))],
        stage=False,
    )
    return attended, grad_q, grad_k, grad_v


def solution(mesh):
    both = P("ctx", "head")
    return jax.shard_map(
        per_device,
        mesh=mesh,
        in_specs=(both, both, both, both, P("ctx"), P("head")),
        out_specs=(both, both, both, both),
        check_vma=False,
    )
```

time: 127 us -> 121 us (0.953)
  Pallas kernels: 16.7 us -> 23.7 us
  local copies, waits for them, and re-layouts: 8.26 us -> 1.65 us
  waiting for transfers between devices: 18.9 us -> 14.2 us
  blocking collectives: 69 us -> 66.7 us
    psum x2 -> x0, blocking collectives: 13 us -> none  [the longest x1 10.6 us: over_heads(): return lax.psum(x, 'head', axis_index_groups=rings)]
    all_to_all x0 -> x1, blocking collectives: none -> 9.72 us  [over_heads(): return lax.all_to_all(parts, 'head', 0, 0, tiled=True).reshape(x.shape)]
    pallas_call x9 -> x10, Pallas kernels: 16.7 us -> 23.7 us  [call(): pl.pallas_call(kernel, name=name, out_shape=[jax.ShapeDtypeStruct(shape,...]
    unnamed x30 -> x12, local copies, waits for them, and re-layouts: 8.26 us -> 1.65 us
    all_to_all x2, waiting for transfers between devices: 18.9 us -> 14.2 us  [exchange(): return lax.all_to_all(parts, 'ctx', 0, 0, tiled=True).reshape(x.shape)]
  transfers between devices with their start and end apart: 2 -> 2, of which waited for: 2 -> 2; matrix products, arithmetic and copies ran while one was open for 0% -> 0% of each run, Pallas kernels for 6% -> 12%
where the time goes in v2:
time: 121 us; the launch traced here: 120 us
  blocking collectives  66.7 us (55%)
  Pallas kernels  23.7 us (20%)
  waiting for transfers between devices  14.2 us (12%)
  starting transfers between devices  13 us (11%)
  local copies, waits for them, and re-layouts  1.65 us (1%)
    all_to_all x2, blocking collectives, exchange(): return lax.all_to_all(parts, 'ctx', 0, 0, tiled=True).reshape(x.shape)  57 us
    pallas_call x10, Pallas kernels, call(): pl.pallas_call(kernel, name=name, out_shape=[jax.ShapeDtypeStruct(shape,...  23.7 us
    all_to_all x2, waiting for transfers between devices, exchange(): return lax.all_to_all(parts, 'ctx', 0, 0, tiled=True).reshape(x.shape)  14.2 us
    all_to_all x2, starting transfers between devices, exchange(): return lax.all_to_all(parts, 'ctx', 0, 0, tiled=True).reshape(x.shape)  13 us
    all_to_all x1, blocking collectives, over_heads(): return lax.all_to_all(parts, 'head', 0, 0, tiled=True).reshape(x.shape)  9.72 us
  transfers between devices with their start and end apart: 2, of which 2 were waited for; matrix products, arithmetic and copies ran while one was open for 0% of the time, Pallas kernels for 12%

profile of v2, /device:TPU:8, one launch (start us, length us, event | category | flops | bytes accessed | tf_op | source)
XLA Modules:
  0.0 120.1 jit_solution(9027041610044355791)
XLA Ops:
  0.6 2.2 %tail.1 = f32[320,128]{1,0:T(8,128)S(1)} custom-call(s32[8,128]{1,0:T(8,128)} %bitcast.20, bf16[1024,256]{1,0:T(8,128)(2,1)} %k_ref.1, bf16[1024,256]{1,0:T(8,128)(2,1)} %v_ref.1), custom_call_target="tpu_custom_call" | custom-call | tf_op jit(solution)/shard_map/tail/pallas_call | solution.py:71
  2.8 35.3 %all_to_all.25 = f32[64,1,640]{2,1,0:T(1,128)S(1)} all-to-all(f32[64,1,640]{2,1,0:T(1,128)S(1)} %bitcast.14), channel_id=1, replica_groups=mesh['head'=8,'ctx'=64] {'ctx'}, dimensions={0} | all-to-all | bytes 327680 | tf_op jit(solution)/shard_map/all_to_all | solution.py:338
  38.1 0.9 before.1
  39.0 6.6 %all-to-all-start.1 = ((f32[64,1,512]{2,1,0:T(1,128)}), f32[64,1,512]{2,1,0:T(1,128)S(1)}, u32[]{:S(2)}, u32[]{:S(2)}) async-start(f32[64,1,512]{2,1,0:T(1,128)} %bitcast.4), calls=%async_computation.1 | async-start | bytes 262144 | tf_op jit(solution)/shard_map/all_to_all | solution.py:338
  45.6 0.0 copy-start.5
  45.6 0.6 copy-done.5
  46.3 4.0 %local.1 = (f32[1024,256]{1,0:T(8,128)S(1)}, bf16[1024,256]{1,0:T(8,128)(2,1)S(1)}, f32[2,128]{1,0:T(2,128)S(1)}) custom-call(bf16[1024,256]{1,0:T(8,128)(2,1)} %refs_0_.5, bf16[1024,256]{1,0:T(8,128)(2,1)} %k_ref.1, bf16[1024,256]{1,0:T(8,128)(2,1)} %v_ref.1, s32[8,128]{1,0:T(8,128)} %bitcast.21, s32[1,1024]{1,0:T(1,128)} %bitcast.22, f32[2]{0:T(128)S(1)} %copy-done.5), custom_call_target="tpu_custom_call" | custom-call | tf_op jit(solution)/shard_map/local/pallas_call | solution.py:71
  50.2 10.2 %all-to-all-done.1 = f32[64,1,512]{2,1,0:T(1,128)S(1)} async-done(((f32[64,1,512]{2,1,0:T(1,128)}), f32[64,1,512]{2,1,0:T(1,128)S(1)}, u32[]{:S(2)}, u32[]{:S(2)}) %all-to-all-start.1) | async-done | bytes 131104 | tf_op jit(solution)/shard_map/all_to_all | solution.py:338
  60.4 0.0 copy-start.3
  60.4 2.6 %attend.1 = (f32[1024,256]{1,0:T(8,128)S(1)}, f32[128,128]{1,0:T(8,128)S(1)}) custom-call(bf16[1024,256]{1,0:T(8,128)(2,1)} %g_ref.1, f32[1024,256]{1,0:T(8,128)S(1)} %get-tuple-element.17.local_ref, bf16[1024,256]{1,0:T(8,128)(2,1)S(1)} %get-tuple-element.18.open_ref, f32[256,128]{1,0:T(8,128)S(1)} %bitcast.12, f32[2,128]{1,0:T(2,128)S(1)} %get-tuple-element.20.gain_ref), custom_call_target="tpu_custom_call" | custom-call | tf_op jit(solution)/shard_map/attend/pallas_call | solution.py:71
  63.0 9.7 %all_to_all.26 = f32[8,1,2048]{2,1,0:T(1,128)S(1)} all-to-all(f32[8,1,2048]{2,1,0:T(1,128)S(1)} %bitcast.28), channel_id=1, replica_groups=mesh['head'=8,'ctx'=64] {'head'}, dimensions={0} | all-to-all | bytes 131072 | tf_op jit(solution)/shard_map/all_to_all | solution.py:343
  72.7 0.0 copy-done.3
  72.7 0.7 inner.1
  73.5 21.7 %all_to_all.27 = f32[64,1,512]{2,1,0:T(1,128)S(1)} all-to-all(f32[64,1,512]{2,1,0:T(1,128)S(1)} %bitcast.27), channel_id=1, replica_groups=mesh['head'=8,'ctx'=64] {'ctx'}, dimensions={0} | all-to-all | bytes 262144 | tf_op jit(solution)/shard_map/all_to_all | solution.py:338
  95.2 0.9 after.1
  96.1 6.4 %all-to-all-start.4 = ((f32[64,1,512]{2,1,0:T(1,128)}), f32[64,1,512]{2,1,0:T(1,128)S(1)}, u32[]{:S(2)}, u32[]{:S(2)}) async-start(f32[64,1,512]{2,1,0:T(1,128)} %bitcast.10), calls=%async_computation.4 | async-start | bytes 262144 | tf_op jit(solution)/shard_map/all_to_all | solution.py:338
  102.5 1.0 attended.1
  103.5 5.2 %near_queries.1 = (bf16[1024,256]{1,0:T(8,128)(2,1)}, f32[1024,256]{1,0:T(8,128)S(1)}) custom-call(bf16[1024,256]{1,0:T(8,128)(2,1)} %refs_0_.5, bf16[1024,256]{1,0:T(8,128)(2,1)} %k_ref.1, bf16[1024,256]{1,0:T(8,128)(2,1)} %v_ref.1, s32[8,128]{1,0:T(8,128)} %bitcast.23, s32[1,1024]{1,0:T(1,128)} %bitcast.24, ...), custom_call_target="tpu_custom_call" | custom-call | tf_op jit(solution)/shard_map/near_queries/pallas_call | solution.py:71
  108.7 0.0 copy-start
  108.8 0.0 copy-start.1
  108.8 0.0 copy-start.4
  108.8 3.7 %near_values.1.values_hbm = f32[1024,256]{1,0:T(8,128)S(1)} custom-call(bf16[1024,256]{1,0:T(8,128)(2,1)} %refs_0_.5, bf16[1024,256]{1,0:T(8,128)(2,1)} %k_ref.1, s32[1,1024]{1,0:T(1,128)} %bitcast.25, bf16[1024,256]{1,0:T(8,128)(2,1)S(1)} %get-tuple-element.23.refs_5_.refs_3_), custom_call_target="tpu_custom_call" | custom-call | tf_op jit(solution)/shard_map/near_values/pallas_call | solution.py:71
  112.5 0.0 copy-start.2
  112.5 1.0 copy-done.2
  113.5 4.0 %all-to-all-done.4 = f32[64,1,512]{2,1,0:T(1,128)S(1)} async-done(((f32[64,1,512]{2,1,0:T(1,128)}), f32[64,1,512]{2,1,0:T(1,128)S(1)}, u32[]{:S(2)}, u32[]{:S(2)}) %all-to-all-start.4) | async-done | bytes 131104 | tf_op jit(solution)/shard_map/all_to_all | solution.py:338
  117.5 0.0 copy-done
  117.5 0.0 copy-done.1
  117.5 0.0 copy-done.4
  117.5 2.4 %far.1 = (bf16[1024,256]{1,0:T(8,128)(2,1)}, bf16[1024,256]{1,0:T(8,128)(2,1)}) custom-call(f32[1024,256]{1,0:T(8,128)} %copy-done.2, bf16[1024,256]{1,0:T(8,128)(2,1)S(1)} %copy-done, bf16[1024,256]{1,0:T(8,128)(2,1)S(1)} %copy-done.1, f32[1024,256]{1,0:T(8,128)S(1)} %get-tuple-element.25.keys_ref, f32[256,128]{1,0:T(8,128)S(1)} %bitcast.18, ...), custom_call_target="tpu_custom_call" | custom-call | tf_op jit(solution)/shard_map/far/pallas_call | solution.py:71
Async XLA Ops:
  39.0 21.4 %all-to-all-start.1 = ((f32[64,1,512]{2,1,0:T(1,128)}), f32[64,1,512]{2,1,0:T(1,128)S(1)}, u32[]{:S(2)}, u32[]{:S(2)}) async-start(f32[64,1,512]{2,1,0:T(1,128)} %bitcast.4), calls=%async_computation.1 | async-start | bytes 262144 | tf_op jit(solution)/shard_map/all_to_all | solution.py:338
  45.6 0.7 copy-start.5
  60.4 12.3 %copy-start.3 = (bf16[1024,256]{1,0:T(8,128)(2,1)S(1)}, bf16[1024,256]{1,0:T(8,128)(2,1)}, u32[]{:S(2)}) copy-start(bf16[1024,256]{1,0:T(8,128)(2,1)} %g_ref.1) | copy-start | bytes 1572868
  96.1 21.4 %all-to-all-start.4 = ((f32[64,1,512]{2,1,0:T(1,128)}), f32[64,1,512]{2,1,0:T(1,128)S(1)}, u32[]{:S(2)}, u32[]{:S(2)}) async-start(f32[64,1,512]{2,1,0:T(1,128)} %bitcast.10), calls=%async_computation.4 | async-start | bytes 262144 | tf_op jit(solution)/shard_map/all_to_all | solution.py:338
  108.7 8.8 %copy-start = (bf16[1024,256]{1,0:T(8,128)(2,1)S(1)}, bf16[1024,256]{1,0:T(8,128)(2,1)}, u32[]{:S(2)}) copy-start(bf16[1024,256]{1,0:T(8,128)(2,1)} %k_ref.1) | copy-start | bytes 1572868
  108.8 8.7 %copy-start.1 = (bf16[1024,256]{1,0:T(8,128)(2,1)S(1)}, bf16[1024,256]{1,0:T(8,128)(2,1)}, u32[]{:S(2)}) copy-start(bf16[1024,256]{1,0:T(8,128)(2,1)} %v_ref.1) | copy-start | bytes 1572868
  108.8 8.7 %copy-start.4 = (s32[1024]{0:T(1024)S(1)}, s32[1024]{0:T(1024)}, u32[]{:S(2)}) copy-start(s32[1024]{0:T(1024)} %param.10) | copy-start | bytes 12292
  112.5 1.0 copy-start.2

commit v3 on v2

--- a/solution.py
+++ b/solution.py
@@ -11,10 +11,11 @@
 
 ROWS = 1024
 LOCAL = 2
-N_CTX = 64
+RING = 16
+N_ROWS = 4
 STEP = 256
 TILES = ROWS // STEP
-CHUNK = LOCAL * HS // N_CTX
+CHUNK = LOCAL * HS // RING
 
 PEERS = 8
 LINES = ROWS // HS
@@ -98,11 +99,11 @@
 def put_state(out_ref, states, stride):
     flat = jnp.concatenate(states, axis=0)
     for r in range(CHUNK):
-        out_ref[pl.ds(r, N_CTX, stride=stride), :] = flat[r * N_CTX : (r + 1) * N_CTX]
+        out_ref[pl.ds(r, RING, stride=stride), :] = flat[r * RING : (r + 1) * RING]
 
 
 def get_state(ref):
-    flat = jnp.concatenate([ref[pl.ds(r, N_CTX, stride=CHUNK), :] for r in range(CHUNK)], axis=0)
+    flat = jnp.concatenate([ref[pl.ds(r, RING, stride=CHUNK), :] for r in range(CHUNK)], axis=0)
     return [flat[h * HS : (h + 1) * HS].astype(BF16) for h in range(LOCAL)]
 
 
@@ -121,8 +122,8 @@
             copy.start()
     seg_copy.wait()
     opening, closing, _, start = marks_of(seg_ref)
-    lane = lax.broadcasted_iota(jnp.int32, (N_CTX, HS), 1)
-    out_ref[pl.ds(CHUNK, N_CTX, stride=CHUNK + 1), :] = jnp.where(lane == 0, opening, closing)
+    lane = lax.broadcasted_iota(jnp.int32, (RING, HS), 1)
+    out_ref[pl.ds(CHUNK, RING, stride=CHUNK + 1), :] = jnp.where(lane == 0, opening, closing) + 1.0
     tails = [jnp.zeros((HS, HS), F32) for _ in range(LOCAL)]
     for i in range(TILES):
         for copy in copies(i):
@@ -135,37 +136,65 @@
     put_state(out_ref, tails, CHUNK + 1)
 
 
-def summed(x_ref, stride, chosen, out_ref):
-    x = jnp.concatenate([x_ref[pl.ds(r, N_CTX, stride=stride), :] for r in range(CHUNK)], axis=1)
+def chunks_of(x_ref, stride, more=None):
+    parts = []
+    for r in range(CHUNK):
+        part = x_ref[pl.ds(r, RING, stride=stride), :]
+        if more is not None:
+            part = jnp.concatenate([part, jnp.broadcast_to(more[r : r + 1], (8, HS))], axis=0)
+        parts.append(part)
+    return jnp.concatenate(parts, axis=1)
+
+
+def summed(chosen, x, out_ref, stride):
     chosen = jnp.where(chosen, 1.0, 0.0).astype(BF16)
     y = dot(jnp.concatenate([chosen] * 3, axis=1), jnp.concatenate(thirds(x), axis=0), (1, 0))
     for r in range(CHUNK):
-        out_ref[pl.ds(r, N_CTX, stride=CHUNK), :] = y[:, r * HS : (r + 1) * HS]
-
-
-def square_iota():
-    shape = (N_CTX, N_CTX)
-    return lax.broadcasted_iota(jnp.int32, shape, 0), lax.broadcasted_iota(jnp.int32, shape, 1)
+        own = y[:, r * HS : (r + 1) * HS]
+        if stride:
+            out_ref[pl.ds(r, RING, stride=stride), :] = own
+        else:
+            out_ref[r : r + 1, :] = own[0:1]
+
+
+def iotas(down, along):
+    return [lax.broadcasted_iota(jnp.int32, (down, along), d) for d in range(2)]
 
 
 def as_row(column):
-    down, along = square_iota()
+    n = column.shape[0]
+    down, along = iotas(n, n)
     return jnp.sum(jnp.where(down == along, column, 0.0), axis=0, keepdims=True)
 
 
-def before_kernel(x_ref, out_ref, marks_ref):
-    marks = x_ref[pl.ds(CHUNK, N_CTX, stride=CHUNK + 1), :]
+def row_end_kernel(x_ref, out_ref, marks_ref):
+    marks = x_ref[pl.ds(CHUNK, RING, stride=CHUNK + 1), :]
     marks_ref[...] = marks
-    down, along = square_iota()
-    chosen = (along < down) & (as_row(marks[:, 1:2]) == marks[:, 0:1])
-    summed(x_ref, CHUNK + 1, chosen, out_ref)
-
-
-def after_kernel(x_ref, marks_ref, out_ref):
-    marks = marks_ref[...]
-    down, along = square_iota()
-    chosen = (along > down) & (as_row(marks[:, 0:1]) == marks[:, 1:2])
-    summed(x_ref, CHUNK, chosen, out_ref)
+    closing = marks[RING - 1 : RING, 1:2]
+    chosen = jnp.broadcast_to(as_row(marks[:, 1:2]) == closing, (8, RING))
+    summed(chosen, chunks_of(x_ref, CHUNK + 1), out_ref, 0)
+    out_ref[CHUNK:, :] = jnp.broadcast_to(closing, (8, HS))
+
+
+def row_start_kernel(x_ref, marks_ref, out_ref):
+    opening = marks_ref[0:1, 0:1]
+    chosen = jnp.broadcast_to(as_row(marks_ref[:, 0:1]) == opening, (8, RING))
+    summed(chosen, chunks_of(x_ref, CHUNK), out_ref, 0)
+    out_ref[CHUNK:, :] = jnp.broadcast_to(opening, (8, HS))
+
+
+def before_kernel(x_ref, marks_ref, more_ref, out_ref):
+    closing = jnp.concatenate([marks_ref[:, 1:2], more_ref[CHUNK:, 0:1]], axis=0)
+    down, along = iotas(RING, RING + 8)
+    chosen = (as_row(closing) == marks_ref[:, 0:1]) & ((along < down) | (along == RING))
+    summed(chosen, chunks_of(x_ref, CHUNK + 1, more_ref[:CHUNK, :]), out_ref, CHUNK)
+
+
+def after_kernel(x_ref, marks_ref, more_ref, out_ref):
+    opening = jnp.concatenate([marks_ref[:, 0:1], more_ref[CHUNK:, 0:1]], axis=0)
+    down, along = iotas(RING, RING + 8)
+    chosen = (as_row(opening) == marks_ref[:, 1:2]) & (along > down) & (along <= RING)
+    summed(chosen, chunks_of(x_ref, CHUNK, more_ref[:CHUNK, :]), out_ref, CHUNK)
 
 
 def column_of(row):
@@ -210,23 +239,30 @@
     for i in range(TILES):
         copy(i).start()
     states = get_state(state_ref)
+
+    def put(n, i, x):
+        line = line_of(x)
+        for j in range(STEP // HS):
+            first = n * LINES + i * (STEP // HS) + j
+            for peer in range(PEERS):
+                row = peer * 2 * LINES + first
+                sums_ref[row : row + 1, :] = line[:, j * HS : (j + 1) * HS]
+
     for i in range(TILES):
         at, reach = i * STEP, (i + 1) * STEP
         power = jnp.zeros((STEP, HS), F32)
-        cross = jnp.zeros((STEP, HS), F32)
-        copy(i).wait()
         for h in range(LOCAL):
             carried = dot(head_of(open_ref, h, at, STEP), states[h], (1, 0))
             scaled = (head_of(local_ref, h, at, STEP) + carried) * gain_ref[h : h + 1, :]
             scaled_ref[at:reach, h * HS : (h + 1) * HS] = scaled
             power = power + scaled * scaled
-            cross = cross + scaled * head_of(g_ref, h, at, STEP).astype(F32)
-        for n, line in enumerate((line_of(power), line_of(cross))):
-            for j in range(STEP // HS):
-                own = line[:, j * HS : (j + 1) * HS]
-                first = n * LINES + i * (STEP // HS) + j
-                for peer in range(PEERS):
-                    sums_ref[peer * 2 * LINES + first : peer * 2 * LINES + first + 1, :] = own
+        put(0, i, power)
+    for i in range(TILES):
+        copy(i).wait()
+        cross = jnp.zeros((STEP, HS), F32)
+        for h in range(LOCAL):
+            cross = cross + head_of(scaled_ref, h, i * STEP, STEP) * head_of(g_ref, h, i * STEP, STEP).astype(F32)
+        put(1, i, cross)
 
 
 def scale_and_pull(sums_ref):
@@ -334,8 +370,15 @@
 
 
 def exchange(x):
-    parts = x.reshape(N_CTX, 1, -1)
-    return lax.all_to_all(parts, "ctx", 0, 0, tiled=True).reshape(x.shape)
+    parts = x.reshape(RING, 1, -1)
+    rings = [[y * RING + z for z in range(RING)] for y in range(N_ROWS)]
+    out = lax.all_to_all(parts, "ctx", 0, 0, axis_index_groups=rings, tiled=True)
+    return out.reshape(x.shape)
+
+
+def to_row(x, by):
+    pairs = [(i, i + by * RING) for i in range(N_ROWS * RING)]
+    return lax.ppermute(x, "ctx", [(a, b) for a, b in pairs if 0 <= b < N_ROWS * RING])
 
 
 def over_heads(x):
@@ -347,9 +390,9 @@
     q, k, v, g, gain = queries, key_vectors, value_vectors, out_grad, head_gain
     seg = segment_ids.reshape(8, HS)
     row = segment_ids.reshape(1, ROWS)
-    states = ((N_CTX * CHUNK, HS), F32)
+    states = ((RING * CHUNK, HS), F32)
     wide, wide_half = ((ROWS, LOCAL * HS), F32), ((ROWS, LOCAL * HS), BF16)
-    payload = ((N_CTX * (CHUNK + 1), HS), F32)
+    payload = ((RING * (CHUNK + 1), HS), F32)
     sums = ((PEERS * 2 * LINES, HS), F32)
     half_stage = pltpu.VMEM(*wide_half)
     two = [half_stage, half_stage, pltpu.SemaphoreType.DMA((2, TILES))]
@@ -363,7 +406,9 @@
     local, q_open, gains = call(
         local_kernel, "local", [wide, wide_half, gains], (q, k, v, seg, row), (gain,), [SMEM]
     )
-    before, marks = call(before_kernel, "before", [states, ((N_CTX, HS), F32)], near=(tails,))
+    carry = ((CHUNK + 8, HS), F32)
+    row_end, marks = call(row_end_kernel, "row_end", [carry, ((RING, HS), F32)], near=(tails,))
+    (before,) = call(before_kernel, "before", [states], near=(tails, marks, to_row(row_end, 1)))
     state_in = exchange(before)
     scaled, part = call(
         attend_kernel,
@@ -380,12 +425,14 @@
     )
     back_tails = exchange(back_tail)
     (attended,) = call(attended_kernel, "attended", [wide_half], near=(scaled, total))
+    (near_v,) = call(near_values_kernel, "near_values", [wide], (q, k, row), (inner,), out_far=1)
     grad_q, near_k = call(
         near_queries_kernel, "near_queries", [wide_half, wide], (q, k, v, seg, row), (inner, state_in)
     )
-    (after,) = call(after_kernel, "after", [states], near=(back_tails, marks))
+    back_tails, near_v, attended = lax.optimization_barrier((back_tails, near_v, attended))
+    (row_start,) = call(row_start_kernel, "row_start", [carry], near=(back_tails, marks))
+    (after,) = call(after_kernel, "after", [states], near=(back_tails, marks, to_row(row_start, -1)))
     state_grad = exchange(after)
-    (near_v,) = call(near_values_kernel, "near_values", [wide], (q, k, row), (inner,), out_far=1)
     grad_k, grad_v = call(
         far_kernel,
         "far",

time: 121 us -> 116 us (0.959)
  the two profiles are of different devices: /device:TPU:8 before, /device:TPU:16 now
where the time goes in v3:
time: 116 us; the launch traced here: 115 us
  blocking collectives  39.6 us (34%)
  waiting for transfers between devices  31.5 us (27%)
  Pallas kernels  24.4 us (21%)
  starting transfers between devices  17.1 us (15%)
  local copies, waits for them, and re-layouts  1.64 us (1%)
    all_to_all x1, blocking collectives, exchange(): lax.all_to_all(parts, 'ctx', 0, 0, axis_index_groups=rings, tiled=True)  29.9 us
    all_to_all x3, waiting for transfers between devices, exchange(): lax.all_to_all(parts, 'ctx', 0, 0, axis_index_groups=rings, tiled=True)  25.9 us
    pallas_call x12, Pallas kernels, call(): pl.pallas_call(kernel, name=name, out_shape=[jax.ShapeDtypeStruct(shape,...  24.4 us
    all_to_all x3, starting transfers between devices, exchange(): lax.all_to_all(parts, 'ctx', 0, 0, axis_index_groups=rings, tiled=True)  11.5 us
    all_to_all x1, blocking collectives, over_heads(): return lax.all_to_all(parts, 'head', 0, 0, tiled=True).reshape(x.shape)  9.72 us
    ppermute x2, waiting for transfers between devices, to_row(): lax.ppermute(x, 'ctx', [(a, b) for a, b in pairs if 0 <= b < N_ROWS * RING])  5.62 us
    ppermute x2, starting transfers between devices, to_row(): lax.ppermute(x, 'ctx', [(a, b) for a, b in pairs if 0 <= b < N_ROWS * RING])  5.54 us
  transfers between devices with their start and end apart: 5, of which 5 were waited for; matrix products, arithmetic and copies ran while one was open for 0% of the time, Pallas kernels for 12%

profile of v3, /device:TPU:16, one launch (start us, length us, event | category | flops | bytes accessed | tf_op | source)
XLA Modules:
  0.0 115.0 jit_solution(10018126987450651578)
XLA Ops:
  0.6 2.2 %tail.1 = f32[272,128]{1,0:T(8,128)S(1)} custom-call(s32[8,128]{1,0:T(8,128)} %bitcast.22, bf16[1024,256]{1,0:T(8,128)(2,1)} %k_ref.1, bf16[1024,256]{1,0:T(8,128)(2,1)} %v_ref.1), custom_call_target="tpu_custom_call" | custom-call | tf_op jit(solution)/shard_map/tail/pallas_call | solution.py:72
  2.8 29.9 %all_to_all.25 = f32[16,1,2176]{2,1,0:T(1,128)S(1)} all-to-all(f32[16,1,2176]{2,1,0:T(1,128)S(1)} %bitcast.20), channel_id=1, replica_groups={{0,1,2,3,4,5,6,7,8,9,10,11,12,13,14,15},{16,17,18,19,20,21,22,23,24,25,..., dimensions={0} | all-to-all | bytes 278528 | tf_op jit(solution)/shard_map/all_to_all | solution.py:375
  32.7 0.3 row_end.1
  33.0 3.2 %collective-permute-start = (f32[24,128]{1,0:T(8,128)S(1)}, f32[24,128]{1,0:T(8,128)S(1)}, u32[]{:S(2)}, u32[]{:S(2)}) collective-permute-start(f32[24,128]{1,0:T(8,128)S(1)} %get-tuple-element.23), channel_id=1, source_target_pairs={{0,16},{1,17},{2,18},{3,19},{4,20},{5,21},{6,22},{7,23},{8,24},{9,... | collective-permute-start | bytes 36872 | tf_op jit(solution)/shard_map/ppermute | solution.py:381
  36.2 2.4 %collective-permute-done.more_ref = f32[24,128]{1,0:T(8,128)S(1)} collective-permute-done((f32[24,128]{1,0:T(8,128)S(1)}, f32[24,128]{1,0:T(8,128)S(1)}, u32[]{:S(2)}, u32[]{:S(2)}) %collective-permute-start) | collective-permute-done | bytes 12320 | tf_op jit(solution)/shard_map/ppermute | solution.py:381
  38.6 1.0 before.1
  39.7 4.0 %all-to-all-start.1 = ((f32[16,1,2048]{2,1,0:T(1,128)}), f32[16,1,2048]{2,1,0:T(1,128)S(1)}, u32[]{:S(2)}, u32[]{:S(2)}) async-start(f32[16,1,2048]{2,1,0:T(1,128)} %bitcast.4), calls=%async_computation.1 | async-start | bytes 262144 | tf_op jit(solution)/shard_map/all_to_all | solution.py:375
  43.6 0.0 copy-start.5
  43.6 0.6 copy-done.5
  44.3 4.0 %local.1 = (f32[1024,256]{1,0:T(8,128)S(1)}, bf16[1024,256]{1,0:T(8,128)(2,1)S(1)}, f32[2,128]{1,0:T(2,128)S(1)}) custom-call(bf16[1024,256]{1,0:T(8,128)(2,1)} %refs_0_.5, bf16[1024,256]{1,0:T(8,128)(2,1)} %k_ref.1, bf16[1024,256]{1,0:T(8,128)(2,1)} %v_ref.1, s32[8,128]{1,0:T(8,128)} %bitcast.23, s32[1,1024]{1,0:T(1,128)} %bitcast.24, f32[2]{0:T(128)S(1)} %copy-done.5), custom_call_target="tpu_custom_call" | custom-call | tf_op jit(solution)/shard_map/local/pallas_call | solution.py:72
  48.2 8.8 %all-to-all-done.1 = f32[16,1,2048]{2,1,0:T(1,128)S(1)} async-done(((f32[16,1,2048]{2,1,0:T(1,128)}), f32[16,1,2048]{2,1,0:T(1,128)S(1)}, u32[]{:S(2)}, u32[]{:S(2)}) %all-to-all-start.1) | async-done | bytes 131104 | tf_op jit(solution)/shard_map/all_to_all | solution.py:375
  57.1 0.0 copy-start.3
  57.1 1.9 %attend.1 = (f32[1024,256]{1,0:T(8,128)S(1)}, f32[128,128]{1,0:T(8,128)S(1)}) custom-call(bf16[1024,256]{1,0:T(8,128)(2,1)} %g_ref.1, f32[1024,256]{1,0:T(8,128)S(1)} %get-tuple-element.20.local_ref, bf16[1024,256]{1,0:T(8,128)(2,1)S(1)} %get-tuple-element.21.open_ref, f32[256,128]{1,0:T(8,128)S(1)} %bitcast.14, f32[2,128]{1,0:T(2,128)S(1)} %get-tuple-element.24.gain_ref), custom_call_target="tpu_custom_call" | custom-call | tf_op jit(solution)/shard_map/attend/pallas_call | solution.py:72
  59.0 9.7 %all_to_all.26 = f32[8,1,2048]{2,1,0:T(1,128)S(1)} all-to-all(f32[8,1,2048]{2,1,0:T(1,128)S(1)} %bitcast.29), channel_id=1, replica_groups=mesh['head'=8,'ctx'=64] {'head'}, dimensions={0} | all-to-all | bytes 131072 | tf_op jit(solution)/shard_map/all_to_all | solution.py:386
  68.8 0.0 copy-done.3
  68.8 1.4 %inner.1 = (bf16[1024,256]{1,0:T(8,128)(2,1)S(1)}, f32[256,128]{1,0:T(8,128)}) custom-call(f32[1024,256]{1,0:T(8,128)S(1)} %get-tuple-element.25.scaled_ref, bf16[1024,256]{1,0:T(8,128)(2,1)S(1)} %copy-done.3, bf16[1024,256]{1,0:T(8,128)(2,1)S(1)} %get-tuple-element.21.open_ref, f32[128,128]{1,0:T(8,128)S(1)} %bitcast.18, ...), custom_call_target="tpu_custom_call" | custom-call | tf_op jit(solution)/shard_map/inner/pallas_call | solution.py:72
  70.2 3.7 %all-to-all-start.3 = ((f32[16,1,2048]{2,1,0:T(1,128)}), f32[16,1,2048]{2,1,0:T(1,128)S(1)}, u32[]{:S(2)}, u32[]{:S(2)}) async-start(f32[16,1,2048]{2,1,0:T(1,128)} %bitcast.8), calls=%async_computation.3 | async-start | bytes 262144 | tf_op jit(solution)/shard_map/all_to_all | solution.py:375
  73.8 1.0 attended.1
  74.9 3.6 %near_values.1.values_hbm = f32[1024,256]{1,0:T(8,128)S(1)} custom-call(bf16[1024,256]{1,0:T(8,128)(2,1)} %refs_0_.5, bf16[1024,256]{1,0:T(8,128)(2,1)} %k_ref.1, s32[1,1024]{1,0:T(1,128)} %bitcast.25, bf16[1024,256]{1,0:T(8,128)(2,1)S(1)} %get-tuple-element.28.refs_3_.refs_5_), custom_call_target="tpu_custom_call" | custom-call | tf_op jit(solution)/shard_map/near_values/pallas_call | solution.py:72
  78.5 0.0 copy-start.2
  78.5 1.0 copy-done.2
  79.5 9.0 %all-to-all-done.3 = f32[16,1,2048]{2,1,0:T(1,128)S(1)} async-done(((f32[16,1,2048]{2,1,0:T(1,128)}), f32[16,1,2048]{2,1,0:T(1,128)S(1)}, u32[]{:S(2)}, u32[]{:S(2)}) %all-to-all-start.3) | async-done | bytes 131104 | tf_op jit(solution)/shard_map/all_to_all | solution.py:375
  88.4 0.3 row_start.1
  88.7 2.4 %collective-permute-start.1 = (f32[24,128]{1,0:T(8,128)S(1)}, f32[24,128]{1,0:T(8,128)S(1)}, u32[]{:S(2)}, u32[]{:S(2)}) collective-permute-start(f32[24,128]{1,0:T(8,128)S(1)} %row_start.1), channel_id=1, source_target_pairs={{16,0},{17,1},{18,2},{19,3},{20,4},{21,5},{22,6},{23,7},{24,8},{25... | collective-permute-start | bytes 36872 | tf_op jit(solution)/shard_map/ppermute | solution.py:381
  91.1 3.2 %collective-permute-done.1.more_ref = f32[24,128]{1,0:T(8,128)S(1)} collective-permute-done((f32[24,128]{1,0:T(8,128)S(1)}, f32[24,128]{1,0:T(8,128)S(1)}, u32[]{:S(2)}, u32[]{:S(2)}) %collective-permute-start.1) | collective-permute-done | bytes 12320 | tf_op jit(solution)/shard_map/ppermute | solution.py:381
  94.3 1.0 after.1
  95.3 3.9 %all-to-all-start.4 = ((f32[16,1,2048]{2,1,0:T(1,128)}), f32[16,1,2048]{2,1,0:T(1,128)S(1)}, u32[]{:S(2)}, u32[]{:S(2)}) async-start(f32[16,1,2048]{2,1,0:T(1,128)} %bitcast.10), calls=%async_computation.4 | async-start | bytes 262144 | tf_op jit(solution)/shard_map/all_to_all | solution.py:375
  99.2 0.0 copy-start
  99.2 0.0 copy-start.1
  99.2 0.0 copy-start.4
  99.2 5.3 %near_queries.1 = (bf16[1024,256]{1,0:T(8,128)(2,1)}, f32[1024,256]{1,0:T(8,128)S(1)}) custom-call(bf16[1024,256]{1,0:T(8,128)(2,1)} %refs_0_.5, bf16[1024,256]{1,0:T(8,128)(2,1)} %k_ref.1, bf16[1024,256]{1,0:T(8,128)(2,1)} %v_ref.1, s32[8,128]{1,0:T(8,128)} %bitcast.26, s32[1,1024]{1,0:T(1,128)} %bitcast.27, ...), custom_call_target="tpu_custom_call" | custom-call | tf_op jit(solution)/shard_map/near_queries/pallas_call | solution.py:72
  104.5 8.1 %all-to-all-done.4 = f32[16,1,2048]{2,1,0:T(1,128)S(1)} async-done(((f32[16,1,2048]{2,1,0:T(1,128)}), f32[16,1,2048]{2,1,0:T(1,128)S(1)}, u32[]{:S(2)}, u32[]{:S(2)}) %all-to-all-start.4) | async-done | bytes 131104 | tf_op jit(solution)/shard_map/all_to_all | solution.py:375
  112.6 0.0 copy-done
  112.6 0.0 copy-done.1
  112.6 0.0 copy-done.4
  112.6 2.4 %far.1 = (bf16[1024,256]{1,0:T(8,128)(2,1)}, bf16[1024,256]{1,0:T(8,128)(2,1)}) custom-call(f32[1024,256]{1,0:T(8,128)} %copy-done.2, bf16[1024,256]{1,0:T(8,128)(2,1)S(1)} %copy-done, bf16[1024,256]{1,0:T(8,128)(2,1)S(1)} %copy-done.1, f32[1024,256]{1,0:T(8,128)S(1)} %get-tuple-element.32.keys_ref, f32[256,128]{1,0:T(8,128)S(1)} %bitcast.21, ...), custom_call_target="tpu_custom_call" | custom-call | tf_op jit(solution)/shard_map/far/pallas_call | solution.py:72
Async XLA Ops:
  33.0 5.6 %collective-permute-start = (f32[24,128]{1,0:T(8,128)S(1)}, f32[24,128]{1,0:T(8,128)S(1)}, u32[]{:S(2)}, u32[]{:S(2)}) collective-permute-start(f32[24,128]{1,0:T(8,128)S(1)} %get-tuple-element.23), channel_id=1, source_target_pairs={{0,16},{1,17},{2,18},{3,19},{4,20},{5,21},{6,22},{7,23},{8,24},{9,... | collective-permute-start | bytes 36872 | tf_op jit(solution)/shard_map/ppermute | solution.py:381
  39.7 17.4 %all-to-all-start.1 = ((f32[16,1,2048]{2,1,0:T(1,128)}), f32[16,1,2048]{2,1,0:T(1,128)S(1)}, u32[]{:S(2)}, u32[]{:S(2)}) async-start(f32[16,1,2048]{2,1,0:T(1,128)} %bitcast.4), calls=%async_computation.1 | async-start | bytes 262144 | tf_op jit(solution)/shard_map/all_to_all | solution.py:375
  43.6 0.7 copy-start.5
  57.1 11.7 %copy-start.3 = (bf16[1024,256]{1,0:T(8,128)(2,1)S(1)}, bf16[1024,256]{1,0:T(8,128)(2,1)}, u32[]{:S(2)}) copy-start(bf16[1024,256]{1,0:T(8,128)(2,1)} %g_ref.1) | copy-start | bytes 1572868
  70.2 18.3 %all-to-all-start.3 = ((f32[16,1,2048]{2,1,0:T(1,128)}), f32[16,1,2048]{2,1,0:T(1,128)S(1)}, u32[]{:S(2)}, u32[]{:S(2)}) async-start(f32[16,1,2048]{2,1,0:T(1,128)} %bitcast.8), calls=%async_computation.3 | async-start | bytes 262144 | tf_op jit(solution)/shard_map/all_to_all | solution.py:375
  78.5 1.0 copy-start.2
  88.7 5.6 %collective-permute-start.1 = (f32[24,128]{1,0:T(8,128)S(1)}, f32[24,128]{1,0:T(8,128)S(1)}, u32[]{:S(2)}, u32[]{:S(2)}) collective-permute-start(f32[24,128]{1,0:T(8,128)S(1)} %row_start.1), channel_id=1, source_target_pairs={{16,0},{17,1},{18,2},{19,3},{20,4},{21,5},{22,6},{23,7},{24,8},{25... | collective-permute-start | bytes 36872 | tf_op jit(solution)/shard_map/ppermute | solution.py:381
  95.3 17.3 %all-to-all-start.4 = ((f32[16,1,2048]{2,1,0:T(1,128)}), f32[16,1,2048]{2,1,0:T(1,128)S(1)}, u32[]{:S(2)}, u32[]{:S(2)}) async-start(f32[16,1,2048]{2,1,0:T(1,128)} %bitcast.10), calls=%async_computation.4 | async-start | bytes 262144 | tf_op jit(solution)/shard_map/all_to_all | solution.py:375
  99.2 13.4 %copy-start = (bf16[1024,256]{1,0:T(8,128)(2,1)S(1)}, bf16[1024,256]{1,0:T(8,128)(2,1)}, u32[]{:S(2)}) copy-start(bf16[1024,256]{1,0:T(8,128)(2,1)} %k_ref.1) | copy-start | bytes 1572868
  99.2 13.4 %copy-start.1 = (bf16[1024,256]{1,0:T(8,128)(2,1)S(1)}, bf16[1024,256]{1,0:T(8,128)(2,1)}, u32[]{:S(2)}) copy-start(bf16[1024,256]{1,0:T(8,128)(2,1)} %v_ref.1) | copy-start | bytes 1572868
  99.2 13.4 %copy-start.4 = (s32[1024]{0:T(1024)S(1)}, s32[1024]{0:T(1024)}, u32[]{:S(2)}) copy-start(s32[1024]{0:T(1024)} %param.10) | copy-start | bytes 12292

commit v4 on v3

--- a/solution.py
+++ b/solution.py
@@ -107,9 +107,13 @@
     return [flat[h * HS : (h + 1) * HS].astype(BF16) for h in range(LOCAL)]
 
 
+TAIL_TILES = 2
+TAIL_STEP = ROWS // TAIL_TILES
+
+
 def tail_kernel(seg_hbm, k_hbm, v_hbm, out_ref, seg_ref, k_ref, v_ref, sems, seg_sem):
     def copies(i):
-        rows = pl.ds(i * STEP, STEP)
+        rows = pl.ds(i * TAIL_STEP, TAIL_STEP)
         return [
             pltpu.make_async_copy(k_hbm.at[rows], k_ref.at[rows], sems.at[0, i]),
             pltpu.make_async_copy(v_hbm.at[rows], v_ref.at[rows], sems.at[1, i]),
@@ -117,7 +121,7 @@
 
     seg_copy = pltpu.make_async_copy(seg_hbm, seg_ref, seg_sem)
     seg_copy.start()
-    for i in range(TILES):
+    for i in range(TAIL_TILES):
         for copy in copies(i):
             copy.start()
     seg_copy.wait()
@@ -125,14 +129,14 @@
     lane = lax.broadcasted_iota(jnp.int32, (RING, HS), 1)
     out_ref[pl.ds(CHUNK, RING, stride=CHUNK + 1), :] = jnp.where(lane == 0, opening, closing) + 1.0
     tails = [jnp.zeros((HS, HS), F32) for _ in range(LOCAL)]
-    for i in range(TILES):
+    for i in range(TAIL_TILES):
         for copy in copies(i):
             copy.wait()
-        at_close = positions(i * STEP, STEP) >= start
-        for h in range(LOCAL):
-            keys = head_of(k_ref, h, i * STEP, STEP).astype(F32)
+        at_close = positions(i * TAIL_STEP, TAIL_STEP) >= start
+        for h in range(LOCAL):
+            keys = head_of(k_ref, h, i * TAIL_STEP, TAIL_STEP).astype(F32)
             keys = jnp.where(at_close, keys, 0.0).astype(BF16)
-            tails[h] = tails[h] + dot(keys, head_of(v_ref, h, i * STEP, STEP), (0, 0))
+            tails[h] = tails[h] + dot(keys, head_of(v_ref, h, i * TAIL_STEP, TAIL_STEP), (0, 0))
     put_state(out_ref, tails, CHUNK + 1)
 
 
@@ -227,8 +231,7 @@
 
 
 def line_of(x):
-    ones = jnp.ones((8, 3 * HS), BF16)
-    return dot(ones, jnp.concatenate(thirds(x), axis=1), (1, 1))[0:1]
+    return jnp.sum(jnp.transpose(x), axis=0, keepdims=True)
 
 
 def attend_kernel(g_hbm, local_ref, open_ref, state_ref, gain_ref, scaled_ref, sums_ref, g_ref, sems):
@@ -240,13 +243,11 @@
         copy(i).start()
     states = get_state(state_ref)
 
+    lines = [[], []]
+
     def put(n, i, x):
         line = line_of(x)
-        for j in range(STEP // HS):
-            first = n * LINES + i * (STEP // HS) + j
-            for peer in range(PEERS):
-                row = peer * 2 * LINES + first
-                sums_ref[row : row + 1, :] = line[:, j * HS : (j + 1) * HS]
+        lines[n] += [line[:, j * HS : (j + 1) * HS] for j in range(STEP // HS)]
 
     for i in range(TILES):
         at, reach = i * STEP, (i + 1) * STEP
@@ -263,6 +264,9 @@
         for h in range(LOCAL):
             cross = cross + head_of(scaled_ref, h, i * STEP, STEP) * head_of(g_ref, h, i * STEP, STEP).astype(F32)
         put(1, i, cross)
+    total = jnp.concatenate(lines[0] + lines[1], axis=0)
+    for peer in range(PEERS):
+        sums_ref[peer * 2 * LINES : (peer + 1) * 2 * LINES, :] = total
 
 
 def scale_and_pull(sums_ref):
@@ -337,14 +341,14 @@
 
 
 def far_kernel(
-    values_hbm, k_ref, v_ref, keys_ref, back_ref, seg_ref, gk_hbm, gv_hbm, values_ref, gk_ref, gv_ref, sems
+    k_hbm, v_ref, keys_ref, values_ref, back_ref, seg_ref, gk_hbm, gv_hbm, k_ref, gk_ref, gv_ref, sems
 ):
     def copy(n, a, b, i):
         rows = pl.ds(i * STEP, STEP)
         return pltpu.make_async_copy(a.at[rows], b.at[rows], sems.at[n, i])
 
     for i in range(TILES):
-        copy(0, values_hbm, values_ref, i).start()
+        copy(0, k_hbm, k_ref, i).start()
     _, _, _, start = marks_of(seg_ref)
     backs = get_state(back_ref)
     for i in range(TILES):
@@ -358,7 +362,7 @@
     for i in range(TILES):
         at, reach = i * STEP, (i + 1) * STEP
         at_close = positions(at, STEP) >= start
-        copy(0, values_hbm, values_ref, i).wait()
+        copy(0, k_hbm, k_ref, i).wait()
         for h in range(LOCAL):
             cols = slice(h * HS, (h + 1) * HS)
             far = jnp.where(at_close, dot(k_ref[at:reach, cols], backs[h], (1, 0)), 0.0)
@@ -425,11 +429,10 @@
     )
     back_tails = exchange(back_tail)
     (attended,) = call(attended_kernel, "attended", [wide_half], near=(scaled, total))
-    (near_v,) = call(near_values_kernel, "near_values", [wide], (q, k, row), (inner,), out_far=1)
+    (near_v,) = call(near_values_kernel, "near_values", [wide], (q, k, row), (inner,))
     grad_q, near_k = call(
         near_queries_kernel, "near_queries", [wide_half, wide], (q, k, v, seg, row), (inner, state_in)
     )
-    back_tails, near_v, attended = lax.optimization_barrier((back_tails, near_v, attended))
     (row_start,) = call(row_start_kernel, "row_start", [carry], near=(back_tails, marks))
     (after,) = call(after_kernel, "after", [states], near=(back_tails, marks, to_row(row_start, -1)))
     state_grad = exchange(after)
@@ -437,10 +440,10 @@
         far_kernel,
         "far",
         [wide_half, wide_half],
-        (near_v,),
-        (k, v, near_k, state_grad, seg),
+        (k,),
+        (v, near_k, near_v, state_grad, seg),
         out_far=2,
-        scratch=[pltpu.VMEM(*wide), half_stage, half_stage, pltpu.SemaphoreType.DMA((3, TILES))],
+        scratch=[half_stage, half_stage, half_stage, pltpu.SemaphoreType.DMA((3, TILES))],
         stage=False,
     )
     return attended, grad_q, grad_k, grad_v

time: 116 us -> 114 us (0.983)
  the two profiles are of different devices: /device:TPU:16 before, /device:TPU:8 now
where the time goes in v4:
time: 114 us; the launch traced here: 113 us
  blocking collectives  57.8 us (51%)
  Pallas kernels  22.7 us (20%)
  waiting for transfers between devices  18.1 us (16%)
  starting transfers between devices  13.1 us (11%)
    all_to_all x2, blocking collectives, exchange(): lax.all_to_all(parts, 'ctx', 0, 0, axis_index_groups=rings, tiled=True)  48.1 us
    pallas_call x12, Pallas kernels, call(): pl.pallas_call(kernel, name=name, out_shape=[jax.ShapeDtypeStruct(shape,...  22.7 us
    all_to_all x2, waiting for transfers between devices, exchange(): lax.all_to_all(parts, 'ctx', 0, 0, axis_index_groups=rings, tiled=True)  12.3 us
    all_to_all x1, blocking collectives, over_heads(): return lax.all_to_all(parts, 'head', 0, 0, tiled=True).reshape(x.shape)  9.73 us
    all_to_all x2, starting transfers between devices, exchange(): lax.all_to_all(parts, 'ctx', 0, 0, axis_index_groups=rings, tiled=True)  7.71 us
    ppermute x2, waiting for transfers between devices, to_row(): lax.ppermute(x, 'ctx', [(a, b) for a, b in pairs if 0 <= b < N_ROWS * RING])  5.75 us
    ppermute x2, starting transfers between devices, to_row(): lax.ppermute(x, 'ctx', [(a, b) for a, b in pairs if 0 <= b < N_ROWS * RING])  5.42 us
  transfers between devices with their start and end apart: 4, of which 4 were waited for; matrix products, arithmetic and copies ran while one was open for 0% of the time, Pallas kernels for 12%

profile of v4, /device:TPU:8, one launch (start us, length us, event | category | flops | bytes accessed | tf_op | source)
XLA Modules:
  0.0 113.1 jit_solution(4705145172160675765)
XLA Ops:
  0.6 1.8 %tail.1 = f32[272,128]{1,0:T(8,128)S(1)} custom-call(s32[8,128]{1,0:T(8,128)} %bitcast.22, bf16[1024,256]{1,0:T(8,128)(2,1)} %k_hbm.3, bf16[1024,256]{1,0:T(8,128)(2,1)} %v_ref.1), custom_call_target="tpu_custom_call" | custom-call | tf_op jit(solution)/shard_map/tail/pallas_call | solution.py:72
  2.4 29.9 %all_to_all.25 = f32[16,1,2176]{2,1,0:T(1,128)S(1)} all-to-all(f32[16,1,2176]{2,1,0:T(1,128)S(1)} %bitcast.20), channel_id=1, replica_groups={{0,1,2,3,4,5,6,7,8,9,10,11,12,13,14,15},{16,17,18,19,20,21,22,23,24,25,..., dimensions={0} | all-to-all | bytes 278528 | tf_op jit(solution)/shard_map/all_to_all | solution.py:379
  32.3 0.3 row_end.1
  32.6 3.5 %collective-permute-start = (f32[24,128]{1,0:T(8,128)S(1)}, f32[24,128]{1,0:T(8,128)S(1)}, u32[]{:S(2)}, u32[]{:S(2)}) collective-permute-start(f32[24,128]{1,0:T(8,128)S(1)} %get-tuple-element.20), channel_id=1, source_target_pairs={{0,16},{1,17},{2,18},{3,19},{4,20},{5,21},{6,22},{7,23},{8,24},{9,... | collective-permute-start | bytes 36872 | tf_op jit(solution)/shard_map/ppermute | solution.py:385
  36.1 2.1 %collective-permute-done.more_ref = f32[24,128]{1,0:T(8,128)S(1)} collective-permute-done((f32[24,128]{1,0:T(8,128)S(1)}, f32[24,128]{1,0:T(8,128)S(1)}, u32[]{:S(2)}, u32[]{:S(2)}) %collective-permute-start) | collective-permute-done | bytes 12320 | tf_op jit(solution)/shard_map/ppermute | solution.py:385
  38.2 1.0 before.1
  39.2 4.0 %all-to-all-start.1 = ((f32[16,1,2048]{2,1,0:T(1,128)}), f32[16,1,2048]{2,1,0:T(1,128)S(1)}, u32[]{:S(2)}, u32[]{:S(2)}) async-start(f32[16,1,2048]{2,1,0:T(1,128)} %bitcast.4), calls=%async_computation.1 | async-start | bytes 262144 | tf_op jit(solution)/shard_map/all_to_all | solution.py:379
  43.2 0.0 copy-start.3
  43.2 0.6 copy-done.3
  43.9 4.0 %local.1 = (f32[1024,256]{1,0:T(8,128)S(1)}, bf16[1024,256]{1,0:T(8,128)(2,1)S(1)}, f32[2,128]{1,0:T(2,128)S(1)}) custom-call(bf16[1024,256]{1,0:T(8,128)(2,1)} %refs_0_.5, bf16[1024,256]{1,0:T(8,128)(2,1)} %k_hbm.3, bf16[1024,256]{1,0:T(8,128)(2,1)} %v_ref.1, s32[8,128]{1,0:T(8,128)} %bitcast.23, s32[1,1024]{1,0:T(1,128)} %bitcast.24, f32[2]{0:T(128)S(1)} %copy-done.3), custom_call_target="tpu_custom_call" | custom-call | tf_op jit(solution)/shard_map/local/pallas_call | solution.py:72
  47.8 8.8 %all-to-all-done.1 = f32[16,1,2048]{2,1,0:T(1,128)S(1)} async-done(((f32[16,1,2048]{2,1,0:T(1,128)}), f32[16,1,2048]{2,1,0:T(1,128)S(1)}, u32[]{:S(2)}, u32[]{:S(2)}) %all-to-all-start.1) | async-done | bytes 131104 | tf_op jit(solution)/shard_map/all_to_all | solution.py:379
  56.7 0.0 copy-start.1
  56.7 1.5 %attend.1 = (f32[1024,256]{1,0:T(8,128)S(1)}, f32[128,128]{1,0:T(8,128)S(1)}) custom-call(bf16[1024,256]{1,0:T(8,128)(2,1)} %g_ref.1, f32[1024,256]{1,0:T(8,128)S(1)} %get-tuple-element.17.local_ref, bf16[1024,256]{1,0:T(8,128)(2,1)S(1)} %get-tuple-element.18.open_ref, f32[256,128]{1,0:T(8,128)S(1)} %bitcast.14, f32[2,128]{1,0:T(2,128)S(1)} %get-tuple-element.21.gain_ref), custom_call_target="tpu_custom_call" | custom-call | tf_op jit(solution)/shard_map/attend/pallas_call | solution.py:72
  58.2 9.7 %all_to_all.26 = f32[8,1,2048]{2,1,0:T(1,128)S(1)} all-to-all(f32[8,1,2048]{2,1,0:T(1,128)S(1)} %bitcast.30), channel_id=1, replica_groups=mesh['head'=8,'ctx'=64] {'head'}, dimensions={0} | all-to-all | bytes 131072 | tf_op jit(solution)/shard_map/all_to_all | solution.py:390
  67.9 0.0 copy-done.1
  67.9 0.7 inner.1
  68.6 18.1 %all_to_all.27 = f32[16,1,2048]{2,1,0:T(1,128)S(1)} all-to-all(f32[16,1,2048]{2,1,0:T(1,128)S(1)} %bitcast.29), channel_id=1, replica_groups={{0,1,2,3,4,5,6,7,8,9,10,11,12,13,14,15},{16,17,18,19,20,21,22,23,24,25,..., dimensions={0} | all-to-all | bytes 262144 | tf_op jit(solution)/shard_map/all_to_all | solution.py:379
  86.8 0.3 row_start.1
  87.1 1.9 %collective-permute-start.1 = (f32[24,128]{1,0:T(8,128)S(1)}, f32[24,128]{1,0:T(8,128)S(1)}, u32[]{:S(2)}, u32[]{:S(2)}) collective-permute-start(f32[24,128]{1,0:T(8,128)S(1)} %row_start.1), channel_id=1, source_target_pairs={{16,0},{17,1},{18,2},{19,3},{20,4},{21,5},{22,6},{23,7},{24,8},{25... | collective-permute-start | bytes 36872 | tf_op jit(solution)/shard_map/ppermute | solution.py:385
  89.0 3.6 %collective-permute-done.1.more_ref = f32[24,128]{1,0:T(8,128)S(1)} collective-permute-done((f32[24,128]{1,0:T(8,128)S(1)}, f32[24,128]{1,0:T(8,128)S(1)}, u32[]{:S(2)}, u32[]{:S(2)}) %collective-permute-start.1) | collective-permute-done | bytes 12320 | tf_op jit(solution)/shard_map/ppermute | solution.py:385
  92.7 1.0 after.1
  93.6 3.7 %all-to-all-start.4 = ((f32[16,1,2048]{2,1,0:T(1,128)}), f32[16,1,2048]{2,1,0:T(1,128)S(1)}, u32[]{:S(2)}, u32[]{:S(2)}) async-start(f32[16,1,2048]{2,1,0:T(1,128)} %bitcast.10), calls=%async_computation.4 | async-start | bytes 262144 | tf_op jit(solution)/shard_map/all_to_all | solution.py:379
  97.4 1.0 attended.1
  98.4 5.2 %near_queries.1 = (bf16[1024,256]{1,0:T(8,128)(2,1)}, f32[1024,256]{1,0:T(8,128)S(1)}) custom-call(bf16[1024,256]{1,0:T(8,128)(2,1)} %refs_0_.5, bf16[1024,256]{1,0:T(8,128)(2,1)} %k_hbm.3, bf16[1024,256]{1,0:T(8,128)(2,1)} %v_ref.1, s32[8,128]{1,0:T(8,128)} %bitcast.25, s32[1,1024]{1,0:T(1,128)} %bitcast.26, ...), custom_call_target="tpu_custom_call" | custom-call | tf_op jit(solution)/shard_map/near_queries/pallas_call | solution.py:72
  103.6 0.0 copy-start
  103.6 0.0 copy-start.2
  103.6 3.6 %near_values.1.values_ref = f32[1024,256]{1,0:T(8,128)S(1)} custom-call(bf16[1024,256]{1,0:T(8,128)(2,1)} %refs_0_.5, bf16[1024,256]{1,0:T(8,128)(2,1)} %k_hbm.3, s32[1,1024]{1,0:T(1,128)} %bitcast.27, bf16[1024,256]{1,0:T(8,128)(2,1)S(1)} %get-tuple-element.24.refs_5_.refs_3_), custom_call_target="tpu_custom_call" | custom-call | tf_op jit(solution)/shard_map/near_values/pallas_call | solution.py:72
  107.3 3.5 %all-to-all-done.4 = f32[16,1,2048]{2,1,0:T(1,128)S(1)} async-done(((f32[16,1,2048]{2,1,0:T(1,128)}), f32[16,1,2048]{2,1,0:T(1,128)S(1)}, u32[]{:S(2)}, u32[]{:S(2)}) %all-to-all-start.4) | async-done | bytes 131104 | tf_op jit(solution)/shard_map/all_to_all | solution.py:379
  110.7 0.0 copy-done
  110.7 0.0 copy-done.2
  110.7 2.4 %far.1 = (bf16[1024,256]{1,0:T(8,128)(2,1)}, bf16[1024,256]{1,0:T(8,128)(2,1)}) custom-call(bf16[1024,256]{1,0:T(8,128)(2,1)} %k_hbm.3, bf16[1024,256]{1,0:T(8,128)(2,1)S(1)} %copy-done, f32[1024,256]{1,0:T(8,128)S(1)} %get-tuple-element.26.keys_ref, f32[1024,256]{1,0:T(8,128)S(1)} %near_values.1.values_ref, f32[256,128]{1,0:T(8,128)S(1)} %bitcast.21, ...), custom_call_target="tpu_custom_call" | custom-call | tf_op jit(solution)/shard_map/far/pallas_call | solution.py:72
Async XLA Ops:
  32.6 5.6 %collective-permute-start = (f32[24,128]{1,0:T(8,128)S(1)}, f32[24,128]{1,0:T(8,128)S(1)}, u32[]{:S(2)}, u32[]{:S(2)}) collective-permute-start(f32[24,128]{1,0:T(8,128)S(1)} %get-tuple-element.20), channel_id=1, source_target_pairs={{0,16},{1,17},{2,18},{3,19},{4,20},{5,21},{6,22},{7,23},{8,24},{9,... | collective-permute-start | bytes 36872 | tf_op jit(solution)/shard_map/ppermute | solution.py:385
  39.2 17.4 %all-to-all-start.1 = ((f32[16,1,2048]{2,1,0:T(1,128)}), f32[16,1,2048]{2,1,0:T(1,128)S(1)}, u32[]{:S(2)}, u32[]{:S(2)}) async-start(f32[16,1,2048]{2,1,0:T(1,128)} %bitcast.4), calls=%async_computation.1 | async-start | bytes 262144 | tf_op jit(solution)/shard_map/all_to_all | solution.py:379
  43.2 0.7 copy-start.3
  56.7 11.2 %copy-start.1 = (bf16[1024,256]{1,0:T(8,128)(2,1)S(1)}, bf16[1024,256]{1,0:T(8,128)(2,1)}, u32[]{:S(2)}) copy-start(bf16[1024,256]{1,0:T(8,128)(2,1)} %g_ref.1) | copy-start | bytes 1572868
  87.1 5.6 %collective-permute-start.1 = (f32[24,128]{1,0:T(8,128)S(1)}, f32[24,128]{1,0:T(8,128)S(1)}, u32[]{:S(2)}, u32[]{:S(2)}) collective-permute-start(f32[24,128]{1,0:T(8,128)S(1)} %row_start.1), channel_id=1, source_target_pairs={{16,0},{17,1},{18,2},{19,3},{20,4},{21,5},{22,6},{23,7},{24,8},{25... | collective-permute-start | bytes 36872 | tf_op jit(solution)/shard_map/ppermute | solution.py:385
  93.6 17.1 %all-to-all-start.4 = ((f32[16,1,2048]{2,1,0:T(1,128)}), f32[16,1,2048]{2,1,0:T(1,128)S(1)}, u32[]{:S(2)}, u32[]{:S(2)}) async-start(f32[16,1,2048]{2,1,0:T(1,128)} %bitcast.10), calls=%async_computation.4 | async-start | bytes 262144 | tf_op jit(solution)/shard_map/all_to_all | solution.py:379
  103.6 7.1 %copy-start = (bf16[1024,256]{1,0:T(8,128)(2,1)S(1)}, bf16[1024,256]{1,0:T(8,128)(2,1)}, u32[]{:S(2)}) copy-start(bf16[1024,256]{1,0:T(8,128)(2,1)} %v_ref.1) | copy-start | bytes 1572868
  103.6 7.1 %copy-start.2 = (s32[1024]{0:T(1024)S(1)}, s32[1024]{0:T(1024)}, u32[]{:S(2)}) copy-start(s32[1024]{0:T(1024)} %param.10) | copy-start | bytes 12292

commit v5 on v4

--- a/solution.py
+++ b/solution.py
@@ -14,6 +14,7 @@
 RING = 16
 N_ROWS = 4
 STEP = 256
+WIDE_STEP = 512
 TILES = ROWS // STEP
 CHUNK = LOCAL * HS // RING
 
@@ -140,14 +141,8 @@
     put_state(out_ref, tails, CHUNK + 1)
 
 
-def chunks_of(x_ref, stride, more=None):
-    parts = []
-    for r in range(CHUNK):
-        part = x_ref[pl.ds(r, RING, stride=stride), :]
-        if more is not None:
-            part = jnp.concatenate([part, jnp.broadcast_to(more[r : r + 1], (8, HS))], axis=0)
-        parts.append(part)
-    return jnp.concatenate(parts, axis=1)
+def chunks_of(x_ref, stride):
+    return jnp.concatenate([x_ref[pl.ds(r, RING, stride=stride), :] for r in range(CHUNK)], axis=1)
 
 
 def summed(chosen, x, out_ref, stride):
@@ -187,18 +182,28 @@
     out_ref[CHUNK:, :] = jnp.broadcast_to(opening, (8, HS))
 
 
-def before_kernel(x_ref, marks_ref, more_ref, out_ref):
-    closing = jnp.concatenate([marks_ref[:, 1:2], more_ref[CHUNK:, 0:1]], axis=0)
-    down, along = iotas(RING, RING + 8)
-    chosen = (as_row(closing) == marks_ref[:, 0:1]) & ((along < down) | (along == RING))
-    summed(chosen, chunks_of(x_ref, CHUNK + 1, more_ref[:CHUNK, :]), out_ref, CHUNK)
-
-
-def after_kernel(x_ref, marks_ref, more_ref, out_ref):
-    opening = jnp.concatenate([marks_ref[:, 0:1], more_ref[CHUNK:, 0:1]], axis=0)
-    down, along = iotas(RING, RING + 8)
-    chosen = (as_row(opening) == marks_ref[:, 1:2]) & (along > down) & (along <= RING)
-    summed(chosen, chunks_of(x_ref, CHUNK, more_ref[:CHUNK, :]), out_ref, CHUNK)
+def before_kernel(x_ref, marks_ref, out_ref):
+    down, along = iotas(RING, RING)
+    chosen = (as_row(marks_ref[:, 1:2]) == marks_ref[:, 0:1]) & (along < down)
+    summed(chosen, chunks_of(x_ref, CHUNK + 1), out_ref, CHUNK)
+
+
+def after_kernel(x_ref, marks_ref, out_ref):
+    down, along = iotas(RING, RING)
+    chosen = (as_row(marks_ref[:, 0:1]) == marks_ref[:, 1:2]) & (along > down)
+    summed(chosen, chunks_of(x_ref, CHUNK), out_ref, CHUNK)
+
+
+def carried_over(side):
+    def kernel(x_ref, marks_ref, more_ref, out_ref):
+        more = more_ref[:CHUNK, :]
+        mark = more_ref[CHUNK : CHUNK + 1, 0:1]
+        for block in range(RING):
+            joined = marks_ref[block : block + 1, side : side + 1] == mark
+            rows = slice(block * CHUNK, (block + 1) * CHUNK)
+            out_ref[rows, :] = x_ref[rows, :] + jnp.where(joined, more, 0.0)
+
+    return kernel
 
 
 def column_of(row):
@@ -236,10 +241,10 @@
 
 def attend_kernel(g_hbm, local_ref, open_ref, state_ref, gain_ref, scaled_ref, sums_ref, g_ref, sems):
     def copy(i):
-        rows = pl.ds(i * STEP, STEP)
+        rows = pl.ds(i * WIDE_STEP, WIDE_STEP)
         return pltpu.make_async_copy(g_hbm.at[rows], g_ref.at[rows], sems.at[i])
 
-    for i in range(TILES):
+    for i in range((ROWS // WIDE_STEP)):
         copy(i).start()
     states = get_state(state_ref)
 
@@ -247,22 +252,22 @@
 
     def put(n, i, x):
         line = line_of(x)
-        lines[n] += [line[:, j * HS : (j + 1) * HS] for j in range(STEP // HS)]
-
-    for i in range(TILES):
-        at, reach = i * STEP, (i + 1) * STEP
-        power = jnp.zeros((STEP, HS), F32)
-        for h in range(LOCAL):
-            carried = dot(head_of(open_ref, h, at, STEP), states[h], (1, 0))
-            scaled = (head_of(local_ref, h, at, STEP) + carried) * gain_ref[h : h + 1, :]
+        lines[n] += [line[:, j * HS : (j + 1) * HS] for j in range(WIDE_STEP // HS)]
+
+    for i in range((ROWS // WIDE_STEP)):
+        at, reach = i * WIDE_STEP, (i + 1) * WIDE_STEP
+        power = jnp.zeros((WIDE_STEP, HS), F32)
+        for h in range(LOCAL):
+            carried = dot(head_of(open_ref, h, at, WIDE_STEP), states[h], (1, 0))
+            scaled = (head_of(local_ref, h, at, WIDE_STEP) + carried) * gain_ref[h : h + 1, :]
             scaled_ref[at:reach, h * HS : (h + 1) * HS] = scaled
             power = power + scaled * scaled
         put(0, i, power)
-    for i in range(TILES):
+    for i in range((ROWS // WIDE_STEP)):
         copy(i).wait()
-        cross = jnp.zeros((STEP, HS), F32)
-        for h in range(LOCAL):
-            cross = cross + head_of(scaled_ref, h, i * STEP, STEP) * head_of(g_ref, h, i * STEP, STEP).astype(F32)
+        cross = jnp.zeros((WIDE_STEP, HS), F32)
+        for h in range(LOCAL):
+            cross = cross + head_of(scaled_ref, h, i * WIDE_STEP, WIDE_STEP) * head_of(g_ref, h, i * WIDE_STEP, WIDE_STEP).astype(F32)
         put(1, i, cross)
     total = jnp.concatenate(lines[0] + lines[1], axis=0)
     for peer in range(PEERS):
@@ -309,8 +314,17 @@
             out_ref[at:reach, cols] = (scaled_ref[at:reach, cols] * scales).astype(BF16)
 
 
-def near_queries_kernel(q_ref, k_ref, v_ref, seg_ref, row_ref, inner_ref, state_ref, gq_ref, keys_ref):
-    _, _, n_open, _ = marks_of(seg_ref)
+def at_close_only(ref, start, out_ref):
+    for h in range(LOCAL):
+        x = jnp.where(positions(0, ROWS) >= start, head_of(ref, h).astype(F32), 0.0)
+        out_ref[:, h * HS : (h + 1) * HS] = x.astype(BF16)
+
+
+def near_queries_kernel(
+    q_ref, k_ref, v_ref, seg_ref, row_ref, inner_ref, state_ref, gq_ref, keys_ref, closing_ref
+):
+    _, _, n_open, start = marks_of(seg_ref)
+    at_close_only(v_ref, start, closing_ref)
     states = get_state(state_ref)
     keys_ref[...] = jnp.zeros(keys_ref.shape, F32)
     for i in range(TILES):
@@ -328,7 +342,9 @@
             keys_ref[:reach, cols] += dot(dprobs, q_ref[at:reach, cols], (0, 0))
 
 
-def near_values_kernel(q_ref, k_ref, row_ref, inner_ref, values_ref):
+def near_values_kernel(q_ref, k_ref, seg_ref, row_ref, inner_ref, values_ref, closing_ref):
+    _, _, _, start = marks_of(seg_ref)
+    at_close_only(k_ref, start, closing_ref)
     values_ref[...] = jnp.zeros(values_ref.shape, F32)
     for i in range(TILES):
         at, reach = i * STEP, (i + 1) * STEP
@@ -341,36 +357,33 @@
 
 
 def far_kernel(
-    k_hbm, v_ref, keys_ref, values_ref, back_ref, seg_ref, gk_hbm, gv_hbm, k_ref, gk_ref, gv_ref, sems
+    k_hbm, v_ref, keys_ref, values_ref, back_ref, gk_hbm, gv_hbm, k_ref, gk_ref, gv_ref, sems, k_sem
 ):
-    def copy(n, a, b, i):
-        rows = pl.ds(i * STEP, STEP)
-        return pltpu.make_async_copy(a.at[rows], b.at[rows], sems.at[n, i])
-
-    for i in range(TILES):
-        copy(0, k_hbm, k_ref, i).start()
-    _, _, _, start = marks_of(seg_ref)
+    fetch = pltpu.make_async_copy(k_hbm, k_ref, k_sem)
+    fetch.start()
     backs = get_state(back_ref)
-    for i in range(TILES):
-        at, reach = i * STEP, (i + 1) * STEP
-        at_close = positions(at, STEP) >= start
-        for h in range(LOCAL):
-            cols = slice(h * HS, (h + 1) * HS)
-            far = jnp.where(at_close, dot(v_ref[at:reach, cols], backs[h], (1, 1)), 0.0)
+    copies = []
+    for i in range(ROWS // WIDE_STEP):
+        at, reach = i * WIDE_STEP, (i + 1) * WIDE_STEP
+        rows = pl.ds(at, WIDE_STEP)
+        for h in range(LOCAL):
+            cols = slice(h * HS, (h + 1) * HS)
+            far = dot(v_ref[at:reach, cols], backs[h], (1, 1))
             gk_ref[at:reach, cols] = (keys_ref[at:reach, cols] + far).astype(BF16)
-        copy(1, gk_ref, gk_hbm, i).start()
-    for i in range(TILES):
-        at, reach = i * STEP, (i + 1) * STEP
-        at_close = positions(at, STEP) >= start
-        copy(0, k_hbm, k_ref, i).wait()
-        for h in range(LOCAL):
-            cols = slice(h * HS, (h + 1) * HS)
-            far = jnp.where(at_close, dot(k_ref[at:reach, cols], backs[h], (1, 0)), 0.0)
+        copies.append(pltpu.make_async_copy(gk_ref.at[rows], gk_hbm.at[rows], sems.at[0, i]))
+        copies[-1].start()
+    fetch.wait()
+    for i in range(ROWS // WIDE_STEP):
+        at, reach = i * WIDE_STEP, (i + 1) * WIDE_STEP
+        rows = pl.ds(at, WIDE_STEP)
+        for h in range(LOCAL):
+            cols = slice(h * HS, (h + 1) * HS)
+            far = dot(k_ref[at:reach, cols], backs[h], (1, 0))
             gv_ref[at:reach, cols] = (values_ref[at:reach, cols] + far).astype(BF16)
-        copy(2, gv_ref, gv_hbm, i).start()
-    for i in range(TILES):
-        copy(1, gk_ref, gk_hbm, i).wait()
-        copy(2, gv_ref, gv_hbm, i).wait()
+        copies.append(pltpu.make_async_copy(gv_ref.at[rows], gv_hbm.at[rows], sems.at[1, i]))
+        copies[-1].start()
+    for copy in copies:
+        copy.wait()
 
 
 def exchange(x):
@@ -412,7 +425,8 @@
     )
     carry = ((CHUNK + 8, HS), F32)
     row_end, marks = call(row_end_kernel, "row_end", [carry, ((RING, HS), F32)], near=(tails,))
-    (before,) = call(before_kernel, "before", [states], near=(tails, marks, to_row(row_end, 1)))
+    (before,) = call(before_kernel, "before", [states], near=(tails, marks))
+    (before,) = call(carried_over(0), "carry_on", [states], near=(before, marks, to_row(row_end, 1)))
     state_in = exchange(before)
     scaled, part = call(
         attend_kernel,
@@ -429,21 +443,22 @@
     )
     back_tails = exchange(back_tail)
     (attended,) = call(attended_kernel, "attended", [wide_half], near=(scaled, total))
-    (near_v,) = call(near_values_kernel, "near_values", [wide], (q, k, row), (inner,))
-    grad_q, near_k = call(
-        near_queries_kernel, "near_queries", [wide_half, wide], (q, k, v, seg, row), (inner, state_in)
+    near_v, k_close = call(near_values_kernel, "near_values", [wide, wide_half], (q, k, seg, row), (inner,), out_far=1)
+    grad_q, near_k, v_close = call(
+        near_queries_kernel, "near_queries", [wide_half, wide, wide_half], (q, k, v, seg, row), (inner, state_in)
     )
     (row_start,) = call(row_start_kernel, "row_start", [carry], near=(back_tails, marks))
-    (after,) = call(after_kernel, "after", [states], near=(back_tails, marks, to_row(row_start, -1)))
+    (after,) = call(after_kernel, "after", [states], near=(back_tails, marks))
+    (after,) = call(carried_over(1), "carry_back", [states], near=(after, marks, to_row(row_start, -1)))
     state_grad = exchange(after)
     grad_k, grad_v = call(
         far_kernel,
         "far",
         [wide_half, wide_half],
-        (k,),
-        (v, near_k, near_v, state_grad, seg),
+        (k_close,),
+        (v_close, near_k, near_v, state_grad),
         out_far=2,
-        scratch=[half_stage, half_stage, half_stage, pltpu.SemaphoreType.DMA((3, TILES))],
+        scratch=[half_stage, *two, pltpu.SemaphoreType.DMA],
         stage=False,
     )
     return attended, grad_q, grad_k, grad_v

time: 114 us -> 113 us (level)
  waiting for transfers between devices: 18.1 us -> 16.5 us
    pallas_call x12 -> x14, Pallas kernels: 22.7 us -> 22.8 us  [call(): pl.pallas_call(kernel, name=name, out_shape=[jax.ShapeDtypeStruct(shape,...]
  transfers between devices with their start and end apart: 4 -> 4, of which waited for: 4 -> 4; matrix products, arithmetic and copies ran while one was open for 0% -> 0% of each run, Pallas kernels for 12% -> 13%
where the time goes in v5:
time: 113 us; the launch traced here: 112 us
  blocking collectives  57.8 us (51%)
  Pallas kernels  22.8 us (20%)
  waiting for transfers between devices  16.5 us (15%)
  starting transfers between devices  13.1 us (12%)
  local copies, waits for them, and re-layouts  1.44 us (1%)
    all_to_all x2, blocking collectives, exchange(): lax.all_to_all(parts, 'ctx', 0, 0, axis_index_groups=rings, tiled=True)  48.1 us
    pallas_call x14, Pallas kernels, call(): pl.pallas_call(kernel, name=name, out_shape=[jax.ShapeDtypeStruct(shape,...  22.8 us
    all_to_all x2, waiting for transfers between devices, exchange(): lax.all_to_all(parts, 'ctx', 0, 0, axis_index_groups=rings, tiled=True)  11.3 us
    all_to_all x1, blocking collectives, over_heads(): return lax.all_to_all(parts, 'head', 0, 0, tiled=True).reshape(x.shape)  9.72 us
    all_to_all x2, starting transfers between devices, exchange(): lax.all_to_all(parts, 'ctx', 0, 0, axis_index_groups=rings, tiled=True)  7.71 us
    ppermute x2, starting transfers between devices, to_row(): lax.ppermute(x, 'ctx', [(a, b) for a, b in pairs if 0 <= b < N_ROWS * RING])  5.42 us
    ppermute x2, waiting for transfers between devices, to_row(): lax.ppermute(x, 'ctx', [(a, b) for a, b in pairs if 0 <= b < N_ROWS * RING])  5.13 us
  transfers between devices with their start and end apart: 4, of which 4 were waited for; matrix products, arithmetic and copies ran while one was open for 0% of the time, Pallas kernels for 13%

profile of v5, /device:TPU:8, one launch (start us, length us, event | category | flops | bytes accessed | tf_op | source)
XLA Modules:
  0.0 112.3 jit_solution(16986257512424927342)
XLA Ops:
  0.6 1.7 %tail.1 = f32[272,128]{1,0:T(8,128)S(1)} custom-call(s32[8,128]{1,0:T(8,128)} %bitcast.24, bf16[1024,256]{1,0:T(8,128)(2,1)} %refs_1_.5, bf16[1024,256]{1,0:T(8,128)(2,1)} %refs_2_.3), custom_call_target="tpu_custom_call" | custom-call | tf_op jit(solution)/shard_map/tail/pallas_call | solution.py:73
  2.4 29.9 %all_to_all.25 = f32[16,1,2176]{2,1,0:T(1,128)S(1)} all-to-all(f32[16,1,2176]{2,1,0:T(1,128)S(1)} %bitcast.20), channel_id=1, replica_groups={{0,1,2,3,4,5,6,7,8,9,10,11,12,13,14,15},{16,17,18,19,20,21,22,23,24,25,..., dimensions={0} | all-to-all | bytes 278528 | tf_op jit(solution)/shard_map/all_to_all | solution.py:392
  32.3 0.3 row_end.1
  32.6 3.5 %collective-permute-start = (f32[24,128]{1,0:T(8,128)S(1)}, f32[24,128]{1,0:T(8,128)S(1)}, u32[]{:S(2)}, u32[]{:S(2)}) collective-permute-start(f32[24,128]{1,0:T(8,128)S(1)} %get-tuple-element.23), channel_id=1, source_target_pairs={{0,16},{1,17},{2,18},{3,19},{4,20},{5,21},{6,22},{7,23},{8,24},{9,... | collective-permute-start | bytes 36872 | tf_op jit(solution)/shard_map/ppermute | solution.py:398
  36.1 0.3 before.1.x_ref
  36.4 1.8 %collective-permute-done.more_ref = f32[24,128]{1,0:T(8,128)S(1)} collective-permute-done((f32[24,128]{1,0:T(8,128)S(1)}, f32[24,128]{1,0:T(8,128)S(1)}, u32[]{:S(2)}, u32[]{:S(2)}) %collective-permute-start) | collective-permute-done | bytes 12320 | tf_op jit(solution)/shard_map/ppermute | solution.py:398
  38.2 0.7 carry_on.1
  38.9 4.0 %all-to-all-start.1 = ((f32[16,1,2048]{2,1,0:T(1,128)}), f32[16,1,2048]{2,1,0:T(1,128)S(1)}, u32[]{:S(2)}, u32[]{:S(2)}) async-start(f32[16,1,2048]{2,1,0:T(1,128)} %bitcast.4), calls=%async_computation.1 | async-start | bytes 262144 | tf_op jit(solution)/shard_map/all_to_all | solution.py:392
  42.8 0.0 copy-start.2
  42.8 0.6 copy-done.2
  43.5 4.0 %local.1 = (f32[1024,256]{1,0:T(8,128)S(1)}, bf16[1024,256]{1,0:T(8,128)(2,1)S(1)}, f32[2,128]{1,0:T(2,128)S(1)}) custom-call(bf16[1024,256]{1,0:T(8,128)(2,1)} %refs_0_.5, bf16[1024,256]{1,0:T(8,128)(2,1)} %refs_1_.5, bf16[1024,256]{1,0:T(8,128)(2,1)} %refs_2_.3, s32[8,128]{1,0:T(8,128)} %bitcast.25, s32[1,1024]{1,0:T(1,128)} %bitcast.26, f32[2]{0:T(128)S(1)} %copy-done.2), custom_call_target="tpu_custom_call" | custom-call | tf_op jit(solution)/shard_map/local/pallas_call | solution.py:73
  47.5 8.9 %all-to-all-done.1 = f32[16,1,2048]{2,1,0:T(1,128)S(1)} async-done(((f32[16,1,2048]{2,1,0:T(1,128)}), f32[16,1,2048]{2,1,0:T(1,128)S(1)}, u32[]{:S(2)}, u32[]{:S(2)}) %all-to-all-start.1) | async-done | bytes 131104 | tf_op jit(solution)/shard_map/all_to_all | solution.py:392
  56.3 0.0 copy-start
  56.3 1.4 %attend.1 = (f32[1024,256]{1,0:T(8,128)S(1)}, f32[128,128]{1,0:T(8,128)S(1)}) custom-call(bf16[1024,256]{1,0:T(8,128)(2,1)} %g_ref.1, f32[1024,256]{1,0:T(8,128)S(1)} %get-tuple-element.20.local_ref, bf16[1024,256]{1,0:T(8,128)(2,1)S(1)} %get-tuple-element.21.open_ref, f32[256,128]{1,0:T(8,128)S(1)} %bitcast.14, f32[2,128]{1,0:T(2,128)S(1)} %get-tuple-element.24.gain_ref), custom_call_target="tpu_custom_call" | custom-call | tf_op jit(solution)/shard_map/attend/pallas_call | solution.py:73
  57.7 9.7 %all_to_all.26 = f32[8,1,2048]{2,1,0:T(1,128)S(1)} all-to-all(f32[8,1,2048]{2,1,0:T(1,128)S(1)} %bitcast.23), channel_id=1, replica_groups=mesh['head'=8,'ctx'=64] {'head'}, dimensions={0} | all-to-all | bytes 131072 | tf_op jit(solution)/shard_map/all_to_all | solution.py:403
  67.4 0.0 copy-done
  67.4 0.7 inner.1
  68.2 18.1 %all_to_all.27 = f32[16,1,2048]{2,1,0:T(1,128)S(1)} all-to-all(f32[16,1,2048]{2,1,0:T(1,128)S(1)} %bitcast.22), channel_id=1, replica_groups={{0,1,2,3,4,5,6,7,8,9,10,11,12,13,14,15},{16,17,18,19,20,21,22,23,24,25,..., dimensions={0} | all-to-all | bytes 262144 | tf_op jit(solution)/shard_map/all_to_all | solution.py:392
  86.3 0.3 row_start.1
  86.6 1.9 %collective-permute-start.1 = (f32[24,128]{1,0:T(8,128)S(1)}, f32[24,128]{1,0:T(8,128)S(1)}, u32[]{:S(2)}, u32[]{:S(2)}) collective-permute-start(f32[24,128]{1,0:T(8,128)S(1)} %row_start.1), channel_id=1, source_target_pairs={{16,0},{17,1},{18,2},{19,3},{20,4},{21,5},{22,6},{23,7},{24,8},{25... | collective-permute-start | bytes 36872 | tf_op jit(solution)/shard_map/ppermute | solution.py:398
  88.5 0.3 after.1.x_ref
  88.8 3.3 %collective-permute-done.1.more_ref = f32[24,128]{1,0:T(8,128)S(1)} collective-permute-done((f32[24,128]{1,0:T(8,128)S(1)}, f32[24,128]{1,0:T(8,128)S(1)}, u32[]{:S(2)}, u32[]{:S(2)}) %collective-permute-start.1) | collective-permute-done | bytes 12320 | tf_op jit(solution)/shard_map/ppermute | solution.py:398
  92.2 0.8 carry_back.1
  93.0 3.7 %all-to-all-start.4 = ((f32[16,1,2048]{2,1,0:T(1,128)}), f32[16,1,2048]{2,1,0:T(1,128)S(1)}, u32[]{:S(2)}, u32[]{:S(2)}) async-start(f32[16,1,2048]{2,1,0:T(1,128)} %bitcast.10), calls=%async_computation.4 | async-start | bytes 262144 | tf_op jit(solution)/shard_map/all_to_all | solution.py:392
  96.8 1.0 attended.1
  97.8 5.2 %near_queries.1 = (bf16[1024,256]{1,0:T(8,128)(2,1)}, f32[1024,256]{1,0:T(8,128)S(1)}, bf16[1024,256]{1,0:T(8,128)(2,1)S(1)}) custom-call(bf16[1024,256]{1,0:T(8,128)(2,1)} %refs_0_.5, bf16[1024,256]{1,0:T(8,128)(2,1)} %refs_1_.5, bf16[1024,256]{1,0:T(8,128)(2,1)} %refs_2_.3, s32[8,128]{1,0:T(8,128)} %bitcast.27, s32[1,1024]{1,0:T(1,128)} %bitcast.28, ...), custom_call_target="tpu_custom_call" | custom-call | tf_op jit(solution)/shard_map/near_queries/pallas_call | solution.py:73
  103.0 3.8 %near_values.1 = (f32[1024,256]{1,0:T(8,128)S(1)}, bf16[1024,256]{1,0:T(8,128)(2,1)S(1)}) custom-call(bf16[1024,256]{1,0:T(8,128)(2,1)} %refs_0_.5, bf16[1024,256]{1,0:T(8,128)(2,1)} %refs_1_.5, s32[8,128]{1,0:T(8,128)} %bitcast.29, s32[1,1024]{1,0:T(1,128)} %bitcast.30, bf16[1024,256]{1,0:T(8,128)(2,1)S(1)} %get-tuple-element.27.refs_5_.refs_4_), custom_call_target="tpu_custom_call" | custom-call | tf_op jit(solution)/shard_map/near_values/pallas_call | solution.py:73
  106.9 0.0 copy-start.1
  106.9 0.8 copy-done.1
  107.7 2.5 %all-to-all-done.4 = f32[16,1,2048]{2,1,0:T(1,128)S(1)} async-done(((f32[16,1,2048]{2,1,0:T(1,128)}), f32[16,1,2048]{2,1,0:T(1,128)S(1)}, u32[]{:S(2)}, u32[]{:S(2)}) %all-to-all-start.4) | async-done | bytes 131104 | tf_op jit(solution)/shard_map/all_to_all | solution.py:392
  110.1 2.2 %far.1 = (bf16[1024,256]{1,0:T(8,128)(2,1)}, bf16[1024,256]{1,0:T(8,128)(2,1)}) custom-call(bf16[1024,256]{1,0:T(8,128)(2,1)} %copy-done.1, bf16[1024,256]{1,0:T(8,128)(2,1)S(1)} %get-tuple-element.30.v_ref, f32[1024,256]{1,0:T(8,128)S(1)} %get-tuple-element.31.keys_ref, f32[1024,256]{1,0:T(8,128)S(1)} %get-tuple-element.32.values_ref, f32[256,128]{1,0:T(8,128)S(1)} %bitcast.21), custom_call_target="tpu_custom_call" | custom-call | tf_op jit(solution)/shard_map/far/pallas_call | solution.py:73
Async XLA Ops:
  32.6 5.6 %collective-permute-start = (f32[24,128]{1,0:T(8,128)S(1)}, f32[24,128]{1,0:T(8,128)S(1)}, u32[]{:S(2)}, u32[]{:S(2)}) collective-permute-start(f32[24,128]{1,0:T(8,128)S(1)} %get-tuple-element.23), channel_id=1, source_target_pairs={{0,16},{1,17},{2,18},{3,19},{4,20},{5,21},{6,22},{7,23},{8,24},{9,... | collective-permute-start | bytes 36872 | tf_op jit(solution)/shard_map/ppermute | solution.py:398
  38.9 17.4 %all-to-all-start.1 = ((f32[16,1,2048]{2,1,0:T(1,128)}), f32[16,1,2048]{2,1,0:T(1,128)S(1)}, u32[]{:S(2)}, u32[]{:S(2)}) async-start(f32[16,1,2048]{2,1,0:T(1,128)} %bitcast.4), calls=%async_computation.1 | async-start | bytes 262144 | tf_op jit(solution)/shard_map/all_to_all | solution.py:392
  42.8 0.7 copy-start.2
  56.3 11.1 %copy-start = (bf16[1024,256]{1,0:T(8,128)(2,1)S(1)}, bf16[1024,256]{1,0:T(8,128)(2,1)}, u32[]{:S(2)}) copy-start(bf16[1024,256]{1,0:T(8,128)(2,1)} %g_ref.1) | copy-start | bytes 1572868
  86.6 5.6 %collective-permute-start.1 = (f32[24,128]{1,0:T(8,128)S(1)}, f32[24,128]{1,0:T(8,128)S(1)}, u32[]{:S(2)}, u32[]{:S(2)}) collective-permute-start(f32[24,128]{1,0:T(8,128)S(1)} %row_start.1), channel_id=1, source_target_pairs={{16,0},{17,1},{18,2},{19,3},{20,4},{21,5},{22,6},{23,7},{24,8},{25... | collective-permute-start | bytes 36872 | tf_op jit(solution)/shard_map/ppermute | solution.py:398
  93.0 17.1 %all-to-all-start.4 = ((f32[16,1,2048]{2,1,0:T(1,128)}), f32[16,1,2048]{2,1,0:T(1,128)S(1)}, u32[]{:S(2)}, u32[]{:S(2)}) async-start(f32[16,1,2048]{2,1,0:T(1,128)} %bitcast.10), calls=%async_computation.4 | async-start | bytes 262144 | tf_op jit(solution)/shard_map/all_to_all | solution.py:392
  106.9 0.8 copy-start.1

commit v6 on v5

--- a/solution.py
+++ b/solution.py
@@ -423,6 +423,7 @@
     local, q_open, gains = call(
         local_kernel, "local", [wide, wide_half, gains], (q, k, v, seg, row), (gain,), [SMEM]
     )
+    tails, local, q_open, gains = lax.optimization_barrier((tails, local, q_open, gains))
     carry = ((CHUNK + 8, HS), F32)
     row_end, marks = call(row_end_kernel, "row_end", [carry, ((RING, HS), F32)], near=(tails,))
     (before,) = call(before_kernel, "before", [states], near=(tails, marks))

time: 113 us -> 113 us (level)
  blocking collectives: 57.8 us -> 45.1 us
  starting transfers between devices: 13.1 us -> 24.4 us
  waiting for transfers between devices: 16.5 us -> 17.9 us
    all_to_all x2, blocking collectives: 48.1 us -> 35.4 us  [exchange(): lax.all_to_all(parts, 'ctx', 0, 0, axis_index_groups=rings, tiled=True)]
    all_to_all x2, starting transfers between devices: 7.71 us -> 19 us  [exchange(): lax.all_to_all(parts, 'ctx', 0, 0, axis_index_groups=rings, tiled=True)]
    all_to_all x2, waiting for transfers between devices: 11.3 us -> 12.8 us  [exchange(): lax.all_to_all(parts, 'ctx', 0, 0, axis_index_groups=rings, tiled=True)]
where the time goes in v6:
time: 113 us; the launch traced here: 112 us
  blocking collectives  45.1 us (40%)
  starting transfers between devices  24.4 us (22%)
  Pallas kernels  22.8 us (20%)
  waiting for transfers between devices  17.9 us (16%)
  local copies, waits for them, and re-layouts  1.44 us (1%)
    all_to_all x2, blocking collectives, exchange(): lax.all_to_all(parts, 'ctx', 0, 0, axis_index_groups=rings, tiled=True)  35.4 us
    pallas_call x14, Pallas kernels, call(): pl.pallas_call(kernel, name=name, out_shape=[jax.ShapeDtypeStruct(shape,...  22.8 us
    all_to_all x2, starting transfers between devices, exchange(): lax.all_to_all(parts, 'ctx', 0, 0, axis_index_groups=rings, tiled=True)  19 us
    all_to_all x2, waiting for transfers between devices, exchange(): lax.all_to_all(parts, 'ctx', 0, 0, axis_index_groups=rings, tiled=True)  12.8 us
    all_to_all x1, blocking collectives, over_heads(): return lax.all_to_all(parts, 'head', 0, 0, tiled=True).reshape(x.shape)  9.72 us
    ppermute x2, starting transfers between devices, to_row(): lax.ppermute(x, 'ctx', [(a, b) for a, b in pairs if 0 <= b < N_ROWS * RING])  5.4 us
    ppermute x2, waiting for transfers between devices, to_row(): lax.ppermute(x, 'ctx', [(a, b) for a, b in pairs if 0 <= b < N_ROWS * RING])  5.14 us
  transfers between devices with their start and end apart: 4, of which 4 were waited for; matrix products, arithmetic and copies ran while one was open for 0% of the time, Pallas kernels for 13%

profile of v6, /device:TPU:8, one launch (start us, length us, event | category | flops | bytes accessed | tf_op | source)
XLA Modules:
  0.0 112.3 jit_solution(17832682306479330249)
XLA Ops:
  0.6 2.4 %tail.1 = f32[272,128]{1,0:T(8,128)} custom-call(s32[8,128]{1,0:T(8,128)} %bitcast.24, bf16[1024,256]{1,0:T(8,128)(2,1)} %refs_1_.5, bf16[1024,256]{1,0:T(8,128)(2,1)} %refs_2_.3), custom_call_target="tpu_custom_call" | custom-call | tf_op jit(solution)/shard_map/tail/pallas_call | solution.py:73
  3.0 15.2 %all-to-all-start = ((f32[16,1,2176]{2,1,0:T(1,128)}), f32[16,1,2176]{2,1,0:T(1,128)S(1)}, u32[]{:S(2)}, u32[]{:S(2)}) async-start(f32[16,1,2176]{2,1,0:T(1,128)} %bitcast.1), calls=%async_computation | async-start | bytes 278528 | tf_op jit(solution)/shard_map/all_to_all | solution.py:392
  18.2 0.0 copy-start.2
  18.3 0.6 copy-done.2
  18.9 4.0 %local.1 = (f32[1024,256]{1,0:T(8,128)S(1)}, bf16[1024,256]{1,0:T(8,128)(2,1)S(1)}, f32[2,128]{1,0:T(2,128)S(1)}) custom-call(bf16[1024,256]{1,0:T(8,128)(2,1)} %refs_0_.5, bf16[1024,256]{1,0:T(8,128)(2,1)} %refs_1_.5, bf16[1024,256]{1,0:T(8,128)(2,1)} %refs_2_.3, s32[8,128]{1,0:T(8,128)} %bitcast.25, s32[1,1024]{1,0:T(1,128)} %bitcast.26, f32[2]{0:T(128)S(1)} %copy-done.2), custom_call_target="tpu_custom_call" | custom-call | tf_op jit(solution)/shard_map/local/pallas_call | solution.py:73
  22.9 10.3 %all-to-all-done = f32[16,1,2176]{2,1,0:T(1,128)S(1)} async-done(((f32[16,1,2176]{2,1,0:T(1,128)}), f32[16,1,2176]{2,1,0:T(1,128)S(1)}, u32[]{:S(2)}, u32[]{:S(2)}) %all-to-all-start) | async-done | bytes 139296 | tf_op jit(solution)/shard_map/all_to_all | solution.py:392
  33.2 0.3 row_end.1
  33.5 3.5 %collective-permute-start = (f32[24,128]{1,0:T(8,128)S(1)}, f32[24,128]{1,0:T(8,128)S(1)}, u32[]{:S(2)}, u32[]{:S(2)}) collective-permute-start(f32[24,128]{1,0:T(8,128)S(1)} %get-tuple-element.31), channel_id=1, source_target_pairs={{0,16},{1,17},{2,18},{3,19},{4,20},{5,21},{6,22},{7,23},{8,24},{9,... | collective-permute-start | bytes 36872 | tf_op jit(solution)/shard_map/ppermute | solution.py:398
  36.9 0.3 before.1.x_ref
  37.2 1.8 %collective-permute-done.more_ref = f32[24,128]{1,0:T(8,128)S(1)} collective-permute-done((f32[24,128]{1,0:T(8,128)S(1)}, f32[24,128]{1,0:T(8,128)S(1)}, u32[]{:S(2)}, u32[]{:S(2)}) %collective-permute-start) | collective-permute-done | bytes 12320 | tf_op jit(solution)/shard_map/ppermute | solution.py:398
  39.0 0.1 carry_on.1
  39.1 17.2 %all_to_all.25 = f32[16,1,2048]{2,1,0:T(1,128)S(1)} all-to-all(f32[16,1,2048]{2,1,0:T(1,128)S(1)} %bitcast.21), channel_id=1, replica_groups={{0,1,2,3,4,5,6,7,8,9,10,11,12,13,14,15},{16,17,18,19,20,21,22,23,24,25,..., dimensions={0} | all-to-all | bytes 262144 | tf_op jit(solution)/shard_map/all_to_all | solution.py:392
  56.3 0.0 copy-start
  56.3 1.4 %attend.1 = (f32[1024,256]{1,0:T(8,128)S(1)}, f32[128,128]{1,0:T(8,128)S(1)}) custom-call(bf16[1024,256]{1,0:T(8,128)(2,1)} %g_ref.1, f32[1024,256]{1,0:T(8,128)S(1)} %get-tuple-element.27.local_ref, bf16[1024,256]{1,0:T(8,128)(2,1)S(1)} %get-tuple-element.28.open_ref, f32[256,128]{1,0:T(8,128)S(1)} %bitcast.14, f32[2,128]{1,0:T(2,128)S(1)} %get-tuple-element.32.gain_ref), custom_call_target="tpu_custom_call" | custom-call | tf_op jit(solution)/shard_map/attend/pallas_call | solution.py:73
  57.7 9.7 %all_to_all.26 = f32[8,1,2048]{2,1,0:T(1,128)S(1)} all-to-all(f32[8,1,2048]{2,1,0:T(1,128)S(1)} %bitcast.23), channel_id=1, replica_groups=mesh['head'=8,'ctx'=64] {'head'}, dimensions={0} | all-to-all | bytes 131072 | tf_op jit(solution)/shard_map/all_to_all | solution.py:403
  67.4 0.0 copy-done
  67.4 0.7 inner.1
  68.2 18.2 %all_to_all.27 = f32[16,1,2048]{2,1,0:T(1,128)S(1)} all-to-all(f32[16,1,2048]{2,1,0:T(1,128)S(1)} %bitcast.22), channel_id=1, replica_groups={{0,1,2,3,4,5,6,7,8,9,10,11,12,13,14,15},{16,17,18,19,20,21,22,23,24,25,..., dimensions={0} | all-to-all | bytes 262144 | tf_op jit(solution)/shard_map/all_to_all | solution.py:392
  86.3 0.3 row_start.1
  86.6 1.9 %collective-permute-start.1 = (f32[24,128]{1,0:T(8,128)S(1)}, f32[24,128]{1,0:T(8,128)S(1)}, u32[]{:S(2)}, u32[]{:S(2)}) collective-permute-start(f32[24,128]{1,0:T(8,128)S(1)} %row_start.1), channel_id=1, source_target_pairs={{16,0},{17,1},{18,2},{19,3},{20,4},{21,5},{22,6},{23,7},{24,8},{25... | collective-permute-start | bytes 36872 | tf_op jit(solution)/shard_map/ppermute | solution.py:398
  88.6 0.3 after.1.x_ref
  88.9 3.4 %collective-permute-done.1.more_ref = f32[24,128]{1,0:T(8,128)S(1)} collective-permute-done((f32[24,128]{1,0:T(8,128)S(1)}, f32[24,128]{1,0:T(8,128)S(1)}, u32[]{:S(2)}, u32[]{:S(2)}) %collective-permute-start.1) | collective-permute-done | bytes 12320 | tf_op jit(solution)/shard_map/ppermute | solution.py:398
  92.2 0.8 carry_back.1
  93.1 3.7 %all-to-all-start.4 = ((f32[16,1,2048]{2,1,0:T(1,128)}), f32[16,1,2048]{2,1,0:T(1,128)S(1)}, u32[]{:S(2)}, u32[]{:S(2)}) async-start(f32[16,1,2048]{2,1,0:T(1,128)} %bitcast.10), calls=%async_computation.4 | async-start | bytes 262144 | tf_op jit(solution)/shard_map/all_to_all | solution.py:392
  96.8 1.0 attended.1
  97.8 5.2 %near_queries.1 = (bf16[1024,256]{1,0:T(8,128)(2,1)}, f32[1024,256]{1,0:T(8,128)S(1)}, bf16[1024,256]{1,0:T(8,128)(2,1)S(1)}) custom-call(bf16[1024,256]{1,0:T(8,128)(2,1)} %refs_0_.5, bf16[1024,256]{1,0:T(8,128)(2,1)} %refs_1_.5, bf16[1024,256]{1,0:T(8,128)(2,1)} %refs_2_.3, s32[8,128]{1,0:T(8,128)} %bitcast.27, s32[1,1024]{1,0:T(1,128)} %bitcast.28, ...), custom_call_target="tpu_custom_call" | custom-call | tf_op jit(solution)/shard_map/near_queries/pallas_call | solution.py:73
  103.1 3.8 %near_values.1 = (f32[1024,256]{1,0:T(8,128)S(1)}, bf16[1024,256]{1,0:T(8,128)(2,1)S(1)}) custom-call(bf16[1024,256]{1,0:T(8,128)(2,1)} %refs_0_.5, bf16[1024,256]{1,0:T(8,128)(2,1)} %refs_1_.5, s32[8,128]{1,0:T(8,128)} %bitcast.29, s32[1,1024]{1,0:T(1,128)} %bitcast.30, bf16[1024,256]{1,0:T(8,128)(2,1)S(1)} %get-tuple-element.35.refs_5_.refs_4_), custom_call_target="tpu_custom_call" | custom-call | tf_op jit(solution)/shard_map/near_values/pallas_call | solution.py:73
  106.9 0.0 copy-start.1
  106.9 0.8 copy-done.1
  107.7 2.5 %all-to-all-done.4 = f32[16,1,2048]{2,1,0:T(1,128)S(1)} async-done(((f32[16,1,2048]{2,1,0:T(1,128)}), f32[16,1,2048]{2,1,0:T(1,128)S(1)}, u32[]{:S(2)}, u32[]{:S(2)}) %all-to-all-start.4) | async-done | bytes 131104 | tf_op jit(solution)/shard_map/all_to_all | solution.py:392
  110.2 2.2 %far.1 = (bf16[1024,256]{1,0:T(8,128)(2,1)}, bf16[1024,256]{1,0:T(8,128)(2,1)}) custom-call(bf16[1024,256]{1,0:T(8,128)(2,1)} %copy-done.1, bf16[1024,256]{1,0:T(8,128)(2,1)S(1)} %get-tuple-element.38.v_ref, f32[1024,256]{1,0:T(8,128)S(1)} %get-tuple-element.39.keys_ref, f32[1024,256]{1,0:T(8,128)S(1)} %get-tuple-element.40.values_ref, f32[256,128]{1,0:T(8,128)S(1)} %bitcast.20), custom_call_target="tpu_custom_call" | custom-call | tf_op jit(solution)/shard_map/far/pallas_call | solution.py:73
Async XLA Ops:
  3.0 30.1 %all-to-all-start = ((f32[16,1,2176]{2,1,0:T(1,128)}), f32[16,1,2176]{2,1,0:T(1,128)S(1)}, u32[]{:S(2)}, u32[]{:S(2)}) async-start(f32[16,1,2176]{2,1,0:T(1,128)} %bitcast.1), calls=%async_computation | async-start | bytes 278528 | tf_op jit(solution)/shard_map/all_to_all | solution.py:392
  18.2 0.7 copy-start.2
  33.5 5.6 %collective-permute-start = (f32[24,128]{1,0:T(8,128)S(1)}, f32[24,128]{1,0:T(8,128)S(1)}, u32[]{:S(2)}, u32[]{:S(2)}) collective-permute-start(f32[24,128]{1,0:T(8,128)S(1)} %get-tuple-element.31), channel_id=1, source_target_pairs={{0,16},{1,17},{2,18},{3,19},{4,20},{5,21},{6,22},{7,23},{8,24},{9,... | collective-permute-start | bytes 36872 | tf_op jit(solution)/shard_map/ppermute | solution.py:398
  56.3 11.1 %copy-start = (bf16[1024,256]{1,0:T(8,128)(2,1)S(1)}, bf16[1024,256]{1,0:T(8,128)(2,1)}, u32[]{:S(2)}) copy-start(bf16[1024,256]{1,0:T(8,128)(2,1)} %g_ref.1) | copy-start | bytes 1572868
  86.6 5.6 %collective-permute-start.1 = (f32[24,128]{1,0:T(8,128)S(1)}, f32[24,128]{1,0:T(8,128)S(1)}, u32[]{:S(2)}, u32[]{:S(2)}) collective-permute-start(f32[24,128]{1,0:T(8,128)S(1)} %row_start.1), channel_id=1, source_target_pairs={{16,0},{17,1},{18,2},{19,3},{20,4},{21,5},{22,6},{23,7},{24,8},{25... | collective-permute-start | bytes 36872 | tf_op jit(solution)/shard_map/ppermute | solution.py:398
  93.1 17.1 %all-to-all-start.4 = ((f32[16,1,2048]{2,1,0:T(1,128)}), f32[16,1,2048]{2,1,0:T(1,128)S(1)}, u32[]{:S(2)}, u32[]{:S(2)}) async-start(f32[16,1,2048]{2,1,0:T(1,128)} %bitcast.10), calls=%async_computation.4 | async-start | bytes 262144 | tf_op jit(solution)/shard_map/all_to_all | solution.py:392
  106.9 0.8 copy-start.1

commit v7 on v6

--- a/solution.py
+++ b/solution.py
@@ -321,8 +321,9 @@
 
 
 def near_queries_kernel(
-    q_ref, k_ref, v_ref, seg_ref, row_ref, inner_ref, state_ref, gq_ref, keys_ref, closing_ref
+    q_ref, k_ref, v_ref, seg_ref, row_ref, inner_ref, state_ref, gq_ref, keys_ref, closing_ref, again_ref
 ):
+    again_ref[...] = inner_ref[...]
     _, _, n_open, start = marks_of(seg_ref)
     at_close_only(v_ref, start, closing_ref)
     states = get_state(state_ref)
@@ -357,10 +358,8 @@
 
 
 def far_kernel(
-    k_hbm, v_ref, keys_ref, values_ref, back_ref, gk_hbm, gv_hbm, k_ref, gk_ref, gv_ref, sems, k_sem
+    k_ref, v_ref, keys_ref, values_ref, back_ref, gk_hbm, gv_hbm, gk_ref, gv_ref, sems
 ):
-    fetch = pltpu.make_async_copy(k_hbm, k_ref, k_sem)
-    fetch.start()
     backs = get_state(back_ref)
     copies = []
     for i in range(ROWS // WIDE_STEP):
@@ -372,7 +371,6 @@
             gk_ref[at:reach, cols] = (keys_ref[at:reach, cols] + far).astype(BF16)
         copies.append(pltpu.make_async_copy(gk_ref.at[rows], gk_hbm.at[rows], sems.at[0, i]))
         copies[-1].start()
-    fetch.wait()
     for i in range(ROWS // WIDE_STEP):
         at, reach = i * WIDE_STEP, (i + 1) * WIDE_STEP
         rows = pl.ds(at, WIDE_STEP)
@@ -444,10 +442,14 @@
     )
     back_tails = exchange(back_tail)
     (attended,) = call(attended_kernel, "attended", [wide_half], near=(scaled, total))
-    near_v, k_close = call(near_values_kernel, "near_values", [wide, wide_half], (q, k, seg, row), (inner,), out_far=1)
-    grad_q, near_k, v_close = call(
-        near_queries_kernel, "near_queries", [wide_half, wide, wide_half], (q, k, v, seg, row), (inner, state_in)
-    )
+    grad_q, near_k, v_close, again = call(
+        near_queries_kernel,
+        "near_queries",
+        [wide_half, wide, wide_half, wide_half],
+        (q, k, v, seg, row),
+        (inner, state_in),
+    )
+    near_v, k_close = call(near_values_kernel, "near_values", [wide, wide_half], (q, k, seg, row), (again,))
     (row_start,) = call(row_start_kernel, "row_start", [carry], near=(back_tails, marks))
     (after,) = call(after_kernel, "after", [states], near=(back_tails, marks))
     (after,) = call(carried_over(1), "carry_back", [states], near=(after, marks, to_row(row_start, -1)))
@@ -456,10 +458,9 @@
         far_kernel,
         "far",
         [wide_half, wide_half],
-        (k_close,),
-        (v_close, near_k, near_v, state_grad),
+        near=(k_close, v_close, near_k, near_v, state_grad),
         out_far=2,
-        scratch=[half_stage, *two, pltpu.SemaphoreType.DMA],
+        scratch=two,
         stage=False,
     )
     return attended, grad_q, grad_k, grad_v

time: 113 us -> 112 us (level)
  no operation moved by 1% of the time
where the time goes in v7:
time: 112 us; the launch traced here: 111 us
  blocking collectives  45.1 us (40%)
  starting transfers between devices  24.4 us (22%)
  Pallas kernels  21.9 us (20%)
  waiting for transfers between devices  18.7 us (17%)
    all_to_all x2, blocking collectives, exchange(): lax.all_to_all(parts, 'ctx', 0, 0, axis_index_groups=rings, tiled=True)  35.4 us
    pallas_call x14, Pallas kernels, call(): pl.pallas_call(kernel, name=name, out_shape=[jax.ShapeDtypeStruct(shape,...  21.9 us
    all_to_all x2, starting transfers between devices, exchange(): lax.all_to_all(parts, 'ctx', 0, 0, axis_index_groups=rings, tiled=True)  19 us
    all_to_all x2, waiting for transfers between devices, exchange(): lax.all_to_all(parts, 'ctx', 0, 0, axis_index_groups=rings, tiled=True)  13.6 us
    all_to_all x1, blocking collectives, over_heads(): return lax.all_to_all(parts, 'head', 0, 0, tiled=True).reshape(x.shape)  9.73 us
    ppermute x2, starting transfers between devices, to_row(): lax.ppermute(x, 'ctx', [(a, b) for a, b in pairs if 0 <= b < N_ROWS * RING])  5.4 us
    ppermute x2, waiting for transfers between devices, to_row(): lax.ppermute(x, 'ctx', [(a, b) for a, b in pairs if 0 <= b < N_ROWS * RING])  5.14 us
  transfers between devices with their start and end apart: 4, of which 4 were waited for; matrix products, arithmetic and copies ran while one was open for 0% of the time, Pallas kernels for 13%

profile of v7, /device:TPU:8, one launch (start us, length us, event | category | flops | bytes accessed | tf_op | source)
XLA Modules:
  0.0 111.5 jit_solution(11105046777622594480)
XLA Ops:
  0.6 2.4 %tail.1 = f32[272,128]{1,0:T(8,128)} custom-call(s32[8,128]{1,0:T(8,128)} %bitcast.24, bf16[1024,256]{1,0:T(8,128)(2,1)} %refs_1_.5, bf16[1024,256]{1,0:T(8,128)(2,1)} %refs_2_.3), custom_call_target="tpu_custom_call" | custom-call | tf_op jit(solution)/shard_map/tail/pallas_call | solution.py:73
  3.1 15.2 %all-to-all-start = ((f32[16,1,2176]{2,1,0:T(1,128)}), f32[16,1,2176]{2,1,0:T(1,128)S(1)}, u32[]{:S(2)}, u32[]{:S(2)}) async-start(f32[16,1,2176]{2,1,0:T(1,128)} %bitcast.1), calls=%async_computation | async-start | bytes 278528 | tf_op jit(solution)/shard_map/all_to_all | solution.py:390
  18.3 0.0 copy-start.1
  18.3 0.6 copy-done.1
  18.9 4.0 %local.1 = (f32[1024,256]{1,0:T(8,128)S(1)}, bf16[1024,256]{1,0:T(8,128)(2,1)S(1)}, f32[2,128]{1,0:T(2,128)S(1)}) custom-call(bf16[1024,256]{1,0:T(8,128)(2,1)} %refs_0_.5, bf16[1024,256]{1,0:T(8,128)(2,1)} %refs_1_.5, bf16[1024,256]{1,0:T(8,128)(2,1)} %refs_2_.3, s32[8,128]{1,0:T(8,128)} %bitcast.25, s32[1,1024]{1,0:T(1,128)} %bitcast.26, f32[2]{0:T(128)S(1)} %copy-done.1), custom_call_target="tpu_custom_call" | custom-call | tf_op jit(solution)/shard_map/local/pallas_call | solution.py:73
  22.9 10.3 %all-to-all-done = f32[16,1,2176]{2,1,0:T(1,128)S(1)} async-done(((f32[16,1,2176]{2,1,0:T(1,128)}), f32[16,1,2176]{2,1,0:T(1,128)S(1)}, u32[]{:S(2)}, u32[]{:S(2)}) %all-to-all-start) | async-done | bytes 139296 | tf_op jit(solution)/shard_map/all_to_all | solution.py:390
  33.2 0.3 row_end.1
  33.5 3.5 %collective-permute-start = (f32[24,128]{1,0:T(8,128)S(1)}, f32[24,128]{1,0:T(8,128)S(1)}, u32[]{:S(2)}, u32[]{:S(2)}) collective-permute-start(f32[24,128]{1,0:T(8,128)S(1)} %get-tuple-element.32), channel_id=1, source_target_pairs={{0,16},{1,17},{2,18},{3,19},{4,20},{5,21},{6,22},{7,23},{8,24},{9,... | collective-permute-start | bytes 36872 | tf_op jit(solution)/shard_map/ppermute | solution.py:396
  37.0 0.3 before.1.x_ref
  37.3 1.8 %collective-permute-done.more_ref = f32[24,128]{1,0:T(8,128)S(1)} collective-permute-done((f32[24,128]{1,0:T(8,128)S(1)}, f32[24,128]{1,0:T(8,128)S(1)}, u32[]{:S(2)}, u32[]{:S(2)}) %collective-permute-start) | collective-permute-done | bytes 12320 | tf_op jit(solution)/shard_map/ppermute | solution.py:396
  39.1 0.1 carry_on.1
  39.1 17.2 %all_to_all.25 = f32[16,1,2048]{2,1,0:T(1,128)S(1)} all-to-all(f32[16,1,2048]{2,1,0:T(1,128)S(1)} %bitcast.21), channel_id=1, replica_groups={{0,1,2,3,4,5,6,7,8,9,10,11,12,13,14,15},{16,17,18,19,20,21,22,23,24,25,..., dimensions={0} | all-to-all | bytes 262144 | tf_op jit(solution)/shard_map/all_to_all | solution.py:390
  56.4 0.0 copy-start
  56.4 1.4 %attend.1 = (f32[1024,256]{1,0:T(8,128)S(1)}, f32[128,128]{1,0:T(8,128)S(1)}) custom-call(bf16[1024,256]{1,0:T(8,128)(2,1)} %g_ref.1, f32[1024,256]{1,0:T(8,128)S(1)} %get-tuple-element.28.local_ref, bf16[1024,256]{1,0:T(8,128)(2,1)S(1)} %get-tuple-element.29.open_ref, f32[256,128]{1,0:T(8,128)S(1)} %bitcast.14, f32[2,128]{1,0:T(2,128)S(1)} %get-tuple-element.33.gain_ref), custom_call_target="tpu_custom_call" | custom-call | tf_op jit(solution)/shard_map/attend/pallas_call | solution.py:73
  57.7 9.7 %all_to_all.26 = f32[8,1,2048]{2,1,0:T(1,128)S(1)} all-to-all(f32[8,1,2048]{2,1,0:T(1,128)S(1)} %bitcast.23), channel_id=1, replica_groups=mesh['head'=8,'ctx'=64] {'head'}, dimensions={0} | all-to-all | bytes 131072 | tf_op jit(solution)/shard_map/all_to_all | solution.py:401
  67.5 0.0 copy-done
  67.5 0.7 inner.1
  68.2 18.2 %all_to_all.27 = f32[16,1,2048]{2,1,0:T(1,128)S(1)} all-to-all(f32[16,1,2048]{2,1,0:T(1,128)S(1)} %bitcast.22), channel_id=1, replica_groups={{0,1,2,3,4,5,6,7,8,9,10,11,12,13,14,15},{16,17,18,19,20,21,22,23,24,25,..., dimensions={0} | all-to-all | bytes 262144 | tf_op jit(solution)/shard_map/all_to_all | solution.py:390
  86.4 0.3 row_start.1
  86.7 1.9 %collective-permute-start.1 = (f32[24,128]{1,0:T(8,128)S(1)}, f32[24,128]{1,0:T(8,128)S(1)}, u32[]{:S(2)}, u32[]{:S(2)}) collective-permute-start(f32[24,128]{1,0:T(8,128)S(1)} %row_start.1), channel_id=1, source_target_pairs={{16,0},{17,1},{18,2},{19,3},{20,4},{21,5},{22,6},{23,7},{24,8},{25... | collective-permute-start | bytes 36872 | tf_op jit(solution)/shard_map/ppermute | solution.py:396
  88.6 0.3 after.1.x_ref
  88.9 3.4 %collective-permute-done.1.more_ref = f32[24,128]{1,0:T(8,128)S(1)} collective-permute-done((f32[24,128]{1,0:T(8,128)S(1)}, f32[24,128]{1,0:T(8,128)S(1)}, u32[]{:S(2)}, u32[]{:S(2)}) %collective-permute-start.1) | collective-permute-done | bytes 12320 | tf_op jit(solution)/shard_map/ppermute | solution.py:396
  92.3 0.8 carry_back.1
  93.1 3.7 %all-to-all-start.4 = ((f32[16,1,2048]{2,1,0:T(1,128)}), f32[16,1,2048]{2,1,0:T(1,128)S(1)}, u32[]{:S(2)}, u32[]{:S(2)}) async-start(f32[16,1,2048]{2,1,0:T(1,128)} %bitcast.10), calls=%async_computation.4 | async-start | bytes 262144 | tf_op jit(solution)/shard_map/all_to_all | solution.py:390
  96.9 1.0 attended.1
  97.9 5.3 %near_queries.1 = (bf16[1024,256]{1,0:T(8,128)(2,1)}, f32[1024,256]{1,0:T(8,128)S(1)}, bf16[1024,256]{1,0:T(8,128)(2,1)S(1)}, bf16[1024,256]{1,0:T(8,128)(2,1)S(1)}) custom-call(bf16[1024,256]{1,0:T(8,128)(2,1)} %refs_0_.5, bf16[1024,256]{1,0:T(8,128)(2,1)} %refs_1_.5, bf16[1024,256]{1,0:T(8,128)(2,1)} %refs_2_.3, s32[8,128]{1,0:T(8,128)} %bitcast.27, ...), custom_call_target="tpu_custom_call" | custom-call | tf_op jit(solution)/shard_map/near_queries/pallas_call | solution.py:73
  103.1 3.8 %near_values.1 = (f32[1024,256]{1,0:T(8,128)S(1)}, bf16[1024,256]{1,0:T(8,128)(2,1)S(1)}) custom-call(bf16[1024,256]{1,0:T(8,128)(2,1)} %refs_0_.5, bf16[1024,256]{1,0:T(8,128)(2,1)} %refs_1_.5, s32[8,128]{1,0:T(8,128)} %bitcast.29, s32[1,1024]{1,0:T(1,128)} %bitcast.30, bf16[1024,256]{1,0:T(8,128)(2,1)S(1)} %get-tuple-element.38.refs_4_), custom_call_target="tpu_custom_call" | custom-call | tf_op jit(solution)/shard_map/near_values/pallas_call | solution.py:73
  106.9 3.3 %all-to-all-done.4 = f32[16,1,2048]{2,1,0:T(1,128)S(1)} async-done(((f32[16,1,2048]{2,1,0:T(1,128)}), f32[16,1,2048]{2,1,0:T(1,128)S(1)}, u32[]{:S(2)}, u32[]{:S(2)}) %all-to-all-start.4) | async-done | bytes 131104 | tf_op jit(solution)/shard_map/all_to_all | solution.py:390
  110.2 1.3 %far.1 = (bf16[1024,256]{1,0:T(8,128)(2,1)}, bf16[1024,256]{1,0:T(8,128)(2,1)}) custom-call(bf16[1024,256]{1,0:T(8,128)(2,1)S(1)} %get-tuple-element.39.k_ref, bf16[1024,256]{1,0:T(8,128)(2,1)S(1)} %get-tuple-element.40.v_ref, f32[1024,256]{1,0:T(8,128)S(1)} %get-tuple-element.41.keys_ref, f32[1024,256]{1,0:T(8,128)S(1)} %get-tuple-element.42.values_ref, ...), custom_call_target="tpu_custom_call" | custom-call | tf_op jit(solution)/shard_map/far/pallas_call | solution.py:73
Async XLA Ops:
  3.1 30.1 %all-to-all-start = ((f32[16,1,2176]{2,1,0:T(1,128)}), f32[16,1,2176]{2,1,0:T(1,128)S(1)}, u32[]{:S(2)}, u32[]{:S(2)}) async-start(f32[16,1,2176]{2,1,0:T(1,128)} %bitcast.1), calls=%async_computation | async-start | bytes 278528 | tf_op jit(solution)/shard_map/all_to_all | solution.py:390
  18.3 0.7 copy-start.1
  33.5 5.6 %collective-permute-start = (f32[24,128]{1,0:T(8,128)S(1)}, f32[24,128]{1,0:T(8,128)S(1)}, u32[]{:S(2)}, u32[]{:S(2)}) collective-permute-start(f32[24,128]{1,0:T(8,128)S(1)} %get-tuple-element.32), channel_id=1, source_target_pairs={{0,16},{1,17},{2,18},{3,19},{4,20},{5,21},{6,22},{7,23},{8,24},{9,... | collective-permute-start | bytes 36872 | tf_op jit(solution)/shard_map/ppermute | solution.py:396
  56.4 11.1 %copy-start = (bf16[1024,256]{1,0:T(8,128)(2,1)S(1)}, bf16[1024,256]{1,0:T(8,128)(2,1)}, u32[]{:S(2)}) copy-start(bf16[1024,256]{1,0:T(8,128)(2,1)} %g_ref.1) | copy-start | bytes 1572868
  86.7 5.6 %collective-permute-start.1 = (f32[24,128]{1,0:T(8,128)S(1)}, f32[24,128]{1,0:T(8,128)S(1)}, u32[]{:S(2)}, u32[]{:S(2)}) collective-permute-start(f32[24,128]{1,0:T(8,128)S(1)} %row_start.1), channel_id=1, source_target_pairs={{16,0},{17,1},{18,2},{19,3},{20,4},{21,5},{22,6},{23,7},{24,8},{25... | collective-permute-start | bytes 36872 | tf_op jit(solution)/shard_map/ppermute | solution.py:396
  93.1 17.1 %all-to-all-start.4 = ((f32[16,1,2048]{2,1,0:T(1,128)}), f32[16,1,2048]{2,1,0:T(1,128)S(1)}, u32[]{:S(2)}, u32[]{:S(2)}) async-start(f32[16,1,2048]{2,1,0:T(1,128)} %bitcast.10), calls=%async_computation.4 | async-start | bytes 262144 | tf_op jit(solution)/shard_map/all_to_all | solution.py:390

commit v8 on v7

--- a/solution.py
+++ b/solution.py
@@ -108,7 +108,7 @@
     return [flat[h * HS : (h + 1) * HS].astype(BF16) for h in range(LOCAL)]
 
 
-TAIL_TILES = 2
+TAIL_TILES = 1
 TAIL_STEP = ROWS // TAIL_TILES
 
 

time: 112 us -> 112 us (level)
  no operation moved by 1% of the time
where the time goes in v8:
time: 112 us; the launch traced here: 111 us
  blocking collectives  45.1 us (40%)
  starting transfers between devices  24.4 us (22%)
  Pallas kernels  21.8 us (19%)
  waiting for transfers between devices  18.7 us (17%)
    all_to_all x2, blocking collectives, exchange(): lax.all_to_all(parts, 'ctx', 0, 0, axis_index_groups=rings, tiled=True)  35.4 us
    pallas_call x14, Pallas kernels, call(): pl.pallas_call(kernel, name=name, out_shape=[jax.ShapeDtypeStruct(shape,...  21.8 us
    all_to_all x2, starting transfers between devices, exchange(): lax.all_to_all(parts, 'ctx', 0, 0, axis_index_groups=rings, tiled=True)  19 us
    all_to_all x2, waiting for transfers between devices, exchange(): lax.all_to_all(parts, 'ctx', 0, 0, axis_index_groups=rings, tiled=True)  13.6 us
    all_to_all x1, blocking collectives, over_heads(): return lax.all_to_all(parts, 'head', 0, 0, tiled=True).reshape(x.shape)  9.72 us
    ppermute x2, starting transfers between devices, to_row(): lax.ppermute(x, 'ctx', [(a, b) for a, b in pairs if 0 <= b < N_ROWS * RING])  5.4 us
    ppermute x2, waiting for transfers between devices, to_row(): lax.ppermute(x, 'ctx', [(a, b) for a, b in pairs if 0 <= b < N_ROWS * RING])  5.14 us
  transfers between devices with their start and end apart: 4, of which 4 were waited for; matrix products, arithmetic and copies ran while one was open for 0% of the time, Pallas kernels for 13%

profile of v8, /device:TPU:8, one launch (start us, length us, event | category | flops | bytes accessed | tf_op | source)
XLA Modules:
  0.0 111.4 jit_solution(4102752976855007747)
XLA Ops:
  0.6 2.3 %tail.1 = f32[272,128]{1,0:T(8,128)} custom-call(s32[8,128]{1,0:T(8,128)} %bitcast.24, bf16[1024,256]{1,0:T(8,128)(2,1)} %refs_1_.5, bf16[1024,256]{1,0:T(8,128)(2,1)} %refs_2_.3), custom_call_target="tpu_custom_call" | custom-call | tf_op jit(solution)/shard_map/tail/pallas_call | solution.py:73
  3.0 15.2 %all-to-all-start = ((f32[16,1,2176]{2,1,0:T(1,128)}), f32[16,1,2176]{2,1,0:T(1,128)S(1)}, u32[]{:S(2)}, u32[]{:S(2)}) async-start(f32[16,1,2176]{2,1,0:T(1,128)} %bitcast.1), calls=%async_computation | async-start | bytes 278528 | tf_op jit(solution)/shard_map/all_to_all | solution.py:390
  18.2 0.0 copy-start.1
  18.2 0.6 copy-done.1
  18.8 4.0 %local.1 = (f32[1024,256]{1,0:T(8,128)S(1)}, bf16[1024,256]{1,0:T(8,128)(2,1)S(1)}, f32[2,128]{1,0:T(2,128)S(1)}) custom-call(bf16[1024,256]{1,0:T(8,128)(2,1)} %refs_0_.5, bf16[1024,256]{1,0:T(8,128)(2,1)} %refs_1_.5, bf16[1024,256]{1,0:T(8,128)(2,1)} %refs_2_.3, s32[8,128]{1,0:T(8,128)} %bitcast.25, s32[1,1024]{1,0:T(1,128)} %bitcast.26, f32[2]{0:T(128)S(1)} %copy-done.1), custom_call_target="tpu_custom_call" | custom-call | tf_op jit(solution)/shard_map/local/pallas_call | solution.py:73
  22.8 10.3 %all-to-all-done = f32[16,1,2176]{2,1,0:T(1,128)S(1)} async-done(((f32[16,1,2176]{2,1,0:T(1,128)}), f32[16,1,2176]{2,1,0:T(1,128)S(1)}, u32[]{:S(2)}, u32[]{:S(2)}) %all-to-all-start) | async-done | bytes 139296 | tf_op jit(solution)/shard_map/all_to_all | solution.py:390
  33.1 0.3 row_end.1
  33.4 3.5 %collective-permute-start = (f32[24,128]{1,0:T(8,128)S(1)}, f32[24,128]{1,0:T(8,128)S(1)}, u32[]{:S(2)}, u32[]{:S(2)}) collective-permute-start(f32[24,128]{1,0:T(8,128)S(1)} %get-tuple-element.32), channel_id=1, source_target_pairs={{0,16},{1,17},{2,18},{3,19},{4,20},{5,21},{6,22},{7,23},{8,24},{9,... | collective-permute-start | bytes 36872 | tf_op jit(solution)/shard_map/ppermute | solution.py:396
  36.9 0.3 before.1.x_ref
  37.2 1.8 %collective-permute-done.more_ref = f32[24,128]{1,0:T(8,128)S(1)} collective-permute-done((f32[24,128]{1,0:T(8,128)S(1)}, f32[24,128]{1,0:T(8,128)S(1)}, u32[]{:S(2)}, u32[]{:S(2)}) %collective-permute-start) | collective-permute-done | bytes 12320 | tf_op jit(solution)/shard_map/ppermute | solution.py:396
  39.0 0.1 carry_on.1
  39.0 17.2 %all_to_all.25 = f32[16,1,2048]{2,1,0:T(1,128)S(1)} all-to-all(f32[16,1,2048]{2,1,0:T(1,128)S(1)} %bitcast.21), channel_id=1, replica_groups={{0,1,2,3,4,5,6,7,8,9,10,11,12,13,14,15},{16,17,18,19,20,21,22,23,24,25,..., dimensions={0} | all-to-all | bytes 262144 | tf_op jit(solution)/shard_map/all_to_all | solution.py:390
  56.3 0.0 copy-start
  56.3 1.4 %attend.1 = (f32[1024,256]{1,0:T(8,128)S(1)}, f32[128,128]{1,0:T(8,128)S(1)}) custom-call(bf16[1024,256]{1,0:T(8,128)(2,1)} %g_ref.1, f32[1024,256]{1,0:T(8,128)S(1)} %get-tuple-element.28.local_ref, bf16[1024,256]{1,0:T(8,128)(2,1)S(1)} %get-tuple-element.29.open_ref, f32[256,128]{1,0:T(8,128)S(1)} %bitcast.14, f32[2,128]{1,0:T(2,128)S(1)} %get-tuple-element.33.gain_ref), custom_call_target="tpu_custom_call" | custom-call | tf_op jit(solution)/shard_map/attend/pallas_call | solution.py:73
  57.6 9.7 %all_to_all.26 = f32[8,1,2048]{2,1,0:T(1,128)S(1)} all-to-all(f32[8,1,2048]{2,1,0:T(1,128)S(1)} %bitcast.23), channel_id=1, replica_groups=mesh['head'=8,'ctx'=64] {'head'}, dimensions={0} | all-to-all | bytes 131072 | tf_op jit(solution)/shard_map/all_to_all | solution.py:401
  67.4 0.0 copy-done
  67.4 0.7 inner.1
  68.1 18.2 %all_to_all.27 = f32[16,1,2048]{2,1,0:T(1,128)S(1)} all-to-all(f32[16,1,2048]{2,1,0:T(1,128)S(1)} %bitcast.22), channel_id=1, replica_groups={{0,1,2,3,4,5,6,7,8,9,10,11,12,13,14,15},{16,17,18,19,20,21,22,23,24,25,..., dimensions={0} | all-to-all | bytes 262144 | tf_op jit(solution)/shard_map/all_to_all | solution.py:390
  86.3 0.3 row_start.1
  86.6 1.9 %collective-permute-start.1 = (f32[24,128]{1,0:T(8,128)S(1)}, f32[24,128]{1,0:T(8,128)S(1)}, u32[]{:S(2)}, u32[]{:S(2)}) collective-permute-start(f32[24,128]{1,0:T(8,128)S(1)} %row_start.1), channel_id=1, source_target_pairs={{16,0},{17,1},{18,2},{19,3},{20,4},{21,5},{22,6},{23,7},{24,8},{25... | collective-permute-start | bytes 36872 | tf_op jit(solution)/shard_map/ppermute | solution.py:396
  88.5 0.3 after.1.x_ref
  88.8 3.4 %collective-permute-done.1.more_ref = f32[24,128]{1,0:T(8,128)S(1)} collective-permute-done((f32[24,128]{1,0:T(8,128)S(1)}, f32[24,128]{1,0:T(8,128)S(1)}, u32[]{:S(2)}, u32[]{:S(2)}) %collective-permute-start.1) | collective-permute-done | bytes 12320 | tf_op jit(solution)/shard_map/ppermute | solution.py:396
  92.2 0.8 carry_back.1
  93.0 3.7 %all-to-all-start.4 = ((f32[16,1,2048]{2,1,0:T(1,128)}), f32[16,1,2048]{2,1,0:T(1,128)S(1)}, u32[]{:S(2)}, u32[]{:S(2)}) async-start(f32[16,1,2048]{2,1,0:T(1,128)} %bitcast.10), calls=%async_computation.4 | async-start | bytes 262144 | tf_op jit(solution)/shard_map/all_to_all | solution.py:390
  96.8 1.0 attended.1
  97.8 5.3 %near_queries.1 = (bf16[1024,256]{1,0:T(8,128)(2,1)}, f32[1024,256]{1,0:T(8,128)S(1)}, bf16[1024,256]{1,0:T(8,128)(2,1)S(1)}, bf16[1024,256]{1,0:T(8,128)(2,1)S(1)}) custom-call(bf16[1024,256]{1,0:T(8,128)(2,1)} %refs_0_.5, bf16[1024,256]{1,0:T(8,128)(2,1)} %refs_1_.5, bf16[1024,256]{1,0:T(8,128)(2,1)} %refs_2_.3, s32[8,128]{1,0:T(8,128)} %bitcast.27, ...), custom_call_target="tpu_custom_call" | custom-call | tf_op jit(solution)/shard_map/near_queries/pallas_call | solution.py:73
  103.0 3.8 %near_values.1 = (f32[1024,256]{1,0:T(8,128)S(1)}, bf16[1024,256]{1,0:T(8,128)(2,1)S(1)}) custom-call(bf16[1024,256]{1,0:T(8,128)(2,1)} %refs_0_.5, bf16[1024,256]{1,0:T(8,128)(2,1)} %refs_1_.5, s32[8,128]{1,0:T(8,128)} %bitcast.29, s32[1,1024]{1,0:T(1,128)} %bitcast.30, bf16[1024,256]{1,0:T(8,128)(2,1)S(1)} %get-tuple-element.38.refs_4_), custom_call_target="tpu_custom_call" | custom-call | tf_op jit(solution)/shard_map/near_values/pallas_call | solution.py:73
  106.8 3.3 %all-to-all-done.4 = f32[16,1,2048]{2,1,0:T(1,128)S(1)} async-done(((f32[16,1,2048]{2,1,0:T(1,128)}), f32[16,1,2048]{2,1,0:T(1,128)S(1)}, u32[]{:S(2)}, u32[]{:S(2)}) %all-to-all-start.4) | async-done | bytes 131104 | tf_op jit(solution)/shard_map/all_to_all | solution.py:390
  110.1 1.3 %far.1 = (bf16[1024,256]{1,0:T(8,128)(2,1)}, bf16[1024,256]{1,0:T(8,128)(2,1)}) custom-call(bf16[1024,256]{1,0:T(8,128)(2,1)S(1)} %get-tuple-element.39.k_ref, bf16[1024,256]{1,0:T(8,128)(2,1)S(1)} %get-tuple-element.40.v_ref, f32[1024,256]{1,0:T(8,128)S(1)} %get-tuple-element.41.keys_ref, f32[1024,256]{1,0:T(8,128)S(1)} %get-tuple-element.42.values_ref, ...), custom_call_target="tpu_custom_call" | custom-call | tf_op jit(solution)/shard_map/far/pallas_call | solution.py:73
Async XLA Ops:
  3.0 30.1 %all-to-all-start = ((f32[16,1,2176]{2,1,0:T(1,128)}), f32[16,1,2176]{2,1,0:T(1,128)S(1)}, u32[]{:S(2)}, u32[]{:S(2)}) async-start(f32[16,1,2176]{2,1,0:T(1,128)} %bitcast.1), calls=%async_computation | async-start | bytes 278528 | tf_op jit(solution)/shard_map/all_to_all | solution.py:390
  18.2 0.7 copy-start.1
  33.4 5.6 %collective-permute-start = (f32[24,128]{1,0:T(8,128)S(1)}, f32[24,128]{1,0:T(8,128)S(1)}, u32[]{:S(2)}, u32[]{:S(2)}) collective-permute-start(f32[24,128]{1,0:T(8,128)S(1)} %get-tuple-element.32), channel_id=1, source_target_pairs={{0,16},{1,17},{2,18},{3,19},{4,20},{5,21},{6,22},{7,23},{8,24},{9,... | collective-permute-start | bytes 36872 | tf_op jit(solution)/shard_map/ppermute | solution.py:396
  56.3 11.1 %copy-start = (bf16[1024,256]{1,0:T(8,128)(2,1)S(1)}, bf16[1024,256]{1,0:T(8,128)(2,1)}, u32[]{:S(2)}) copy-start(bf16[1024,256]{1,0:T(8,128)(2,1)} %g_ref.1) | copy-start | bytes 1572868
  86.6 5.6 %collective-permute-start.1 = (f32[24,128]{1,0:T(8,128)S(1)}, f32[24,128]{1,0:T(8,128)S(1)}, u32[]{:S(2)}, u32[]{:S(2)}) collective-permute-start(f32[24,128]{1,0:T(8,128)S(1)} %row_start.1), channel_id=1, source_target_pairs={{16,0},{17,1},{18,2},{19,3},{20,4},{21,5},{22,6},{23,7},{24,8},{25... | collective-permute-start | bytes 36872 | tf_op jit(solution)/shard_map/ppermute | solution.py:396
  93.0 17.1 %all-to-all-start.4 = ((f32[16,1,2048]{2,1,0:T(1,128)}), f32[16,1,2048]{2,1,0:T(1,128)S(1)}, u32[]{:S(2)}, u32[]{:S(2)}) async-start(f32[16,1,2048]{2,1,0:T(1,128)} %bitcast.10), calls=%async_computation.4 | async-start | bytes 262144 | tf_op jit(solution)/shard_map/all_to_all | solution.py:390
